TPU v7x, 32 devices: a whole 2x2x4 slice. The times are simulated.
32 devices in a mesh: row: 4 (over y, x), col: 8 (over z, core).
Axes of the slice: x: 2, y: 2, z: 4, core: 2. Of those that a mesh axis runs over, the one named last changes fastest.
Arguments:
- intensity: float32 [16, 2048, 2048], P(None, 'row', 'col'), may hold values from -6 to 6
- punch_radius: int32 [2, 129, 129], replicated, may hold values from 0 to 12
Outputs:
- out_re: float32 [16, 2048, 2048], P(None, ('row', 'col'))
- out_im: float32 [16, 2048, 2048], P(None, ('row', 'col'))
Inputs may be any that keep to these rules, and one draw needn't show every extreme that they name: `punch_radius`: squared radius in voxels; 0 leaves a node unpunched.
All inputs are finite; a program needn't handle non-finite values.
Results may differ from a plain program's by a relative error of at most 0.0029.
Values may be sent and summed in bfloat16 or wider, within the bound.
A program may use at most 128 MiB of HBM per device.

v0:
```python
import math

import jax
import jax.numpy as jnp
from jax import lax
from jax.sharding import PartitionSpec as P

N = 2048
SP = 16


def circle(count, period, width):
    first_ids = jnp.arange(count, dtype=jnp.int32)
    second_ids = jnp.arange(width, dtype=jnp.int32)
    phases = first_ids[:, None] * second_ids[None, :] % period
    angles = phases.astype(jnp.float32) * (2.0 * math.pi / period)
    return (jnp.cos(angles), jnp.sin(angles))


def mixed(form, left, right):
    return jnp.einsum(form, left, right, precision=lax.Precision.HIGHEST)


def spectral(real_in, imag_in):
    length = real_in.shape[-1]
    first = 32
    second = length // first
    shape_lead = real_in.shape[:-1]
    cos_first, sin_first = circle(first, first, first)
    cos_twist, sin_twist = circle(first, length, second)
    cos_second, sin_second = circle(second, second, second)
    grid_re = real_in.reshape(shape_lead + (first, second))
    section_re = mixed("...ab,ac->...cb", grid_re, cos_first)
    section_im = mixed("...ab,ac->...cb", grid_re, sin_first)
    grid_im = imag_in.reshape(shape_lead + (first, second))
    section_re = section_re - mixed("...ab,ac->...cb", grid_im, sin_first)
    section_im = section_im + mixed("...ab,ac->...cb", grid_im, cos_first)
    twist_re = section_re * cos_twist - section_im * sin_twist
    twist_im = section_re * sin_twist + section_im * cos_twist
    final_re = mixed("...cb,bd->...dc", twist_re, cos_second) - mixed(
        "...cb,bd->...dc", twist_im, sin_second
    )
    final_im = mixed("...cb,bd->...dc", twist_re, sin_second) + mixed(
        "...cb,bd->...dc", twist_im, cos_second
    )
    return (final_re.reshape(shape_lead + (length,)), final_im.reshape(shape_lead + (length,)))


def spectral_lead(real_in):
    row_total, length = real_in.shape
    first = 32
    second = length // first
    cos_first, sin_first = circle(first, first, first)
    cos_twist, sin_twist = circle(first, length, second)
    cos_second, sin_second = circle(second, second, second)
    grid_re = real_in.reshape(row_total, first, second)
    section_re = mixed("rab,ac->cbr", grid_re, cos_first)
    section_im = mixed("rab,ac->cbr", grid_re, sin_first)
    twist_re = section_re * cos_twist[:, :, None] - section_im * sin_twist[:, :, None]
    twist_im = section_re * sin_twist[:, :, None] + section_im * cos_twist[:, :, None]
    final_re = mixed("cbr,bd->dcr", twist_re, cos_second) - mixed(
        "cbr,bd->dcr", twist_im, sin_second
    )
    final_im = mixed("cbr,bd->dcr", twist_re, sin_second) + mixed(
        "cbr,bd->dcr", twist_im, cos_second
    )
    return (final_re.reshape(length, row_total), final_im.reshape(length, row_total))


def keep_map(first_coords, second_coords, radius_table, levels):
    node_count = radius_table.shape[1]
    first_node = (first_coords + SP // 2) // SP
    first_dist = first_coords - SP * first_node
    second_node = (second_coords + SP // 2) // SP
    second_dist = second_coords - SP * second_node
    plane_node = (levels + SP // 2) // SP
    plane_dist = levels - SP * plane_node
    node_ids = jnp.arange(node_count, dtype=jnp.int32)
    pick_first = (first_node[:, None] == node_ids[None, :]).astype(jnp.bfloat16)
    pick_second = (second_node[:, None] == node_ids[None, :]).astype(jnp.bfloat16)
    table_half = jnp.einsum(
        "hn,snm->shm",
        pick_first,
        radius_table.astype(jnp.bfloat16),
        preferred_element_type=jnp.float32,
    ).astype(jnp.bfloat16)
    plane_radius = jnp.einsum(
        "shm,km->shk", table_half, pick_second, preferred_element_type=jnp.float32
    )
    level_ids = jnp.arange(radius_table.shape[0], dtype=jnp.int32)
    pick_plane = (plane_node[:, None] == level_ids[None, :]).astype(jnp.float32)
    radius = jnp.einsum("ls,shk->hlk", pick_plane, plane_radius, precision=lax.Precision.HIGHEST)
    distance = (
        (first_dist * first_dist)[:, None, None]
        + (plane_dist * plane_dist)[None, :, None]
        + (second_dist * second_dist)[None, None, :]
    )
    return (distance.astype(jnp.float32) >= radius).astype(jnp.float32)


def body(intensity, punch_radius):
    row_count = lax.axis_size("row")
    col_count = lax.axis_size("col")
    row_at = lax.axis_index("row")
    col_at = lax.axis_index("col")
    planes, h_block, k_block = intensity.shape
    groups = col_count // row_count
    fine_width = k_block // col_count
    pencil_rows = groups * fine_width
    levels = jnp.arange(planes, dtype=jnp.int32)
    swapped_table = jnp.swapaxes(punch_radius, 1, 2)
    outgoing = jnp.transpose(
        intensity.reshape(planes, h_block, col_count, fine_width), (2, 3, 0, 1)
    )
    arrived = lax.all_to_all(
        lax.all_to_all(outgoing, "col", split_axis=0, concat_axis=0, tiled=True),
        "row",
        split_axis=0,
        concat_axis=3,
        tiled=True,
    )
    pencil_h = (
        h_block * row_at
        + k_block * jnp.arange(groups, dtype=jnp.int32)[:, None]
        + fine_width * col_at
        + jnp.arange(fine_width, dtype=jnp.int32)[None, :]
    ).reshape(-1)
    whole_k = jnp.arange(N, dtype=jnp.int32)
    mirrored = arrived.reshape(pencil_rows, planes, N)
    pencil_input = jnp.transpose(
        intensity.reshape(planes, groups, col_count, fine_width, k_block), (1, 2, 3, 0, 4)
    )
    direct = lax.all_to_all(pencil_input, "col", split_axis=1, concat_axis=4, tiled=True).reshape(
        pencil_rows, planes, N
    )
    keep_mask = keep_map(pencil_h, whole_k, punch_radius, levels)
    keep_swap = keep_map(pencil_h, whole_k, swapped_table, levels)
    counts = jnp.maximum(keep_mask + keep_swap, 1.0)
    symmetric = ((keep_mask * direct + keep_swap * mirrored) / counts).astype(jnp.bfloat16)
    row_total = pencil_rows * planes
    flat_rows = symmetric.reshape(row_total, N).astype(jnp.float32)
    part_re, part_im = spectral_lead(flat_rows)
    freq_width = N // (row_count * col_count)
    sectioned = jnp.stack([part_re, part_im]).reshape(
        2, row_count, col_count, freq_width, row_total
    )
    spectra = lax.all_to_all(
        lax.all_to_all(sectioned, "row", split_axis=1, concat_axis=1, tiled=True),
        "col",
        split_axis=2,
        concat_axis=2,
        tiled=True,
    )
    spectra = spectra.reshape(2, row_count, col_count, freq_width, groups, fine_width, planes)
    spectra = jnp.transpose(spectra, (0, 6, 3, 1, 4, 2, 5)).reshape(2, planes * freq_width, N)
    final_re, final_im = spectral(spectra[0], spectra[1])
    out_re = (final_re / N).reshape(planes, freq_width, N)
    out_im = (final_im / N).reshape(planes, freq_width, N)
    return (out_re, out_im)


def solution(mesh):
    in_specs = (P(None, "row", "col"), P())
    out_specs = (P(None, ("row", "col"), None), P(None, ("row", "col"), None))
    return jax.shard_map(body, mesh=mesh, in_specs=in_specs, out_specs=out_specs, check_vma=False)
```

profile of v0, /device:TPU:0, one launch (start us, length us, event | category | flops | bytes accessed | tf_op | source)
XLA Modules:
  0.0 1491.7 jit_solution(7893386067648535456)
XLA Ops:
  0.6 13.3 copy.78
  13.9 6.4 all-to-all-start
  20.3 9.2 copy.82
  29.5 8.6 copy.83
  38.1 166.1 %all-to-all-done = f32[2,8,32,16,256]{4,3,2,0,1:T(8,128)} async-done(((f32[2,8,32,16,256]{4,3,2,0,1:T(8,128)}), f32[2,8,32,16,256]{4,3,2,0,1:T(8,128)}, u32[]{:S(2)}, u32[]{:S(2)}) %all-to-all-start) | async-done | bytes 8388640 | tf_op jit(solution)/shard_map/all_to_all | solution.py:133
  204.2 189.6 %all_to_all.45 = f32[8,32,16,512]{3,1,2,0:T(8,128)} all-to-all(f32[8,32,16,512]{3,1,2,0:T(8,128)} %copy.83), channel_id=1, replica_groups=mesh['row'=4,'col'=8] {'col'}, dimensions={0} | all-to-all | bytes 16777216 | tf_op jit(solution)/shard_map/all_to_all | solution.py:116
  393.8 6.0 all-to-all-start.2
  399.8 0.1 iota_add_fusion.1
  399.9 0.1 add.277
  400.0 0.0 copy-done.3
  400.0 0.1 convert_element_type.106
  400.1 0.1 fusion.90
  400.3 0.0 copy-start.4
  400.3 0.0 copy-start.6
  400.3 0.1 broadcast_add_fusion
  400.4 0.1 convert_bitcast_fusion
  400.5 0.5 fusion.37
  401.0 0.5 fusion.36
  401.5 7.5 fusion.42
  409.0 14.9 copy.79
  423.9 9.7 reshape.301
  433.5 58.5 %all-to-all-done.2 = f32[8,32,16,512]{3,1,2,0:T(8,128)} async-done(((f32[8,32,16,512]{3,1,2,0:T(8,128)}), f32[8,32,16,512]{3,1,2,0:T(8,128)}, u32[]{:S(2)}, u32[]{:S(2)}) %all-to-all-start.2) | async-done | bytes 8388640 | tf_op jit(solution)/shard_map/all_to_all | solution.py:115
  492.0 12.2 copy.85
  504.2 10.9 reshape.303
  515.1 13.7 divide_convert_fusion
  528.8 12.8 reshape.304
  541.7 12.0 copy.86
  553.6 9.2 fusion.84
  562.9 0.0 copy-done.4
  562.9 0.0 copy-done.6
  562.9 0.0 copy-done.2
  562.9 7.6 subtract_bitcast_fusion.1
  570.4 11.9 fusion.16
  582.4 13.6 fusion.18
  596.0 13.8 fusion.24
  609.8 13.4 fusion.27
  623.2 8.2 copy.93
  631.4 8.3 copy.90
  639.7 4.9 pad_maximum_fusion
  644.6 2.1 copy.94
  646.7 185.4 %all_to_all.46 = f32[2,4,8,64,1024]{4,3,2,0,1:T(8,128)S(1)} all-to-all(f32[2,4,8,64,1024]{4,3,2,0,1:T(8,128)S(1)} %copy.94), channel_id=1, replica_groups=mesh['row'=4,'col'=8] {'row'}, dimensions={1} | all-to-all | bytes 33554432 | tf_op jit(solution)/shard_map/all_to_all | solution.py:148
  832.0 2.1 copy.95
  834.2 368.5 %all_to_all.47 = f32[2,4,8,64,1024]{4,3,1,0,2:T(8,128)} all-to-all(f32[2,4,8,64,1024]{4,3,1,0,2:T(8,128)S(1)} %copy.95), channel_id=1, replica_groups=mesh['row'=4,'col'=8] {'col'}, dimensions={2} | all-to-all | bytes 33554432 | tf_op jit(solution)/shard_map/all_to_all | solution.py:147
  1202.6 22.9 %copy.96 = f32[2,4,8,64,1024]{3,4,2,1,0:T(8,128)} copy(f32[2,4,8,64,1024]{4,3,1,0,2:T(8,128)} %all_to_all.47) | data formatting | bytes 33554432 | tf_op jit(solution)/shard_map/all_to_all | solution.py:147
  1225.6 17.9 %fusion.183 = (f32[1,16,64,4,2,8,32]{2,1,6,4,5,3,0:T(8,128)S(1)}, f32[1,16,64,4,2,8,32]{2,1,6,4,5,3,0:T(8,128)}) fusion(f32[2,16,64,4,2,8,32]{2,1,6,4,5,3,0:T(8,128)} %bitcast.116), kind=kLoop, calls=%fused_computation.195 | loop fusion | bytes 33554432 | tf_op jit(solution)/shard_map/slice | solution.py:156
  1243.4 6.0 copy.99
  1249.5 14.5 reshape_squeeze.7
  1263.9 17.3 %fusion.8 = f32[32,1024,64]{1,0,2:T(8,128)} fusion(f32[1024,32,64]{0,2,1:T(8,128)} %reshape_squeeze.7), kind=kOutput, calls=%fused_computation.18 | convolution fusion | flops 805320704 | bytes 16777216 | tf_op jit(solution)/shard_map/...ab,ac->...cb/dot_general | solution.py:21
  1281.2 13.6 fusion.10
  1294.8 11.5 copy.97
  1306.2 14.5 reshape_squeeze.6
  1320.7 17.4 %fusion.12 = f32[32,1024,64]{1,0,2:T(8,128)} fusion(f32[1024,32,64]{0,2,1:T(8,128)} %reshape_squeeze.6), kind=kOutput, calls=%fused_computation.22 | convolution fusion | flops 805320704 | bytes 16777216 | tf_op jit(solution)/shard_map/...ab,ac->...cb/dot_general | solution.py:21
  1338.1 24.2 %subtract_bitcast_fusion = (f32[1024,32,64]{0,1,2:T(8,128)}, f32[1024,32,64]{0,1,2:T(8,128)}) fusion(f32[32,64]{0,1:T(8,128)S(1)} %copy-done.5, f32[32,64]{0,1:T(8,128)S(1)} %copy-done.7, f32[32,1024,64]{1,0,2:T(8,128)} %fusion.12, f32[32,1024,64]{1,0,2:T(8,128)} %fusion.8, f32[32,1024,64]{1,0,2:T(8,128)} %fusion.10, f32[1024,32,64]{0,2,1:T(8,128)} %reshape_squeeze.6), kind=kOutput, calls=%fused_computation.6 | convolution fusion | flops 822097920 | bytes 50348032 | tf_op jit(solution)/shard_map/...ab,ac->...cb/dot_general | solution.py:21
  1362.4 15.9 %fusion = f32[64,1024,32]{1,0,2:T(8,128)S(1)} fusion(f32[1024,32,64]{0,1,2:T(8,128)} %get-tuple-element.11), kind=kOutput, calls=%fused_computation.10 | convolution fusion | flops 1610670080 | bytes 16777216 | tf_op jit(solution)/shard_map/...cb,bd->...dc/dot_general | solution.py:21
  1378.3 0.0 slice-start.1
  1378.3 13.7 fusion.2
  1392.0 14.0 multiply_bitcast_fusion.1
  1406.0 13.7 multiply_bitcast_fusion
  1419.7 11.5 copy.108
  1431.2 8.3 copy.105
  1439.4 13.3 div.98
  1452.7 12.7 copy.109
  1465.4 13.3 div.101
  1478.8 12.7 copy.110
  (20 shorter events, 0.1 us)
Async XLA Ops:
  13.9 190.3 %all-to-all-start = ((f32[2,8,32,16,256]{4,3,2,0,1:T(8,128)}), f32[2,8,32,16,256]{4,3,2,0,1:T(8,128)}, u32[]{:S(2)}, u32[]{:S(2)}) async-start(f32[2,8,32,16,256]{4,3,2,0,1:T(8,128)} %copy.78), calls=%async_computation | async-start | bytes 16777216 | tf_op jit(solution)/shard_map/all_to_all | solution.py:133
  393.8 6.2 copy-start.3
  393.8 98.2 %all-to-all-start.2 = ((f32[8,32,16,512]{3,1,2,0:T(8,128)}), f32[8,32,16,512]{3,1,2,0:T(8,128)}, u32[]{:S(2)}, u32[]{:S(2)}) async-start(f32[8,32,16,512]{3,1,2,0:T(8,128)} %all_to_all.45), calls=%async_computation.2 | async-start | bytes 16777216 | tf_op jit(solution)/shard_map/all_to_all | solution.py:115
  400.3 162.6 %copy-start.4 = (f32[32,64]{0,1:T(8,128)}, f32[32,64]{0,1:T(8,128)S(1)}, u32[]{:S(2)}) copy-start(f32[32,64]{0,1:T(8,128)S(1)} %get-tuple-element.16) | copy-start | bytes 24580
  400.3 162.6 %copy-start.6 = (f32[32,64]{0,1:T(8,128)}, f32[32,64]{0,1:T(8,128)S(1)}, u32[]{:S(2)}) copy-start(f32[32,64]{0,1:T(8,128)S(1)} %get-tuple-element.17) | copy-start | bytes 24580
  553.6 9.2 copy-start.2
  1263.9 17.3 %copy-start = (f32[1024,32,64]{0,2,1:T(8,128)S(1)}, f32[1024,32,64]{0,2,1:T(8,128)}, u32[]{:S(2)}) copy-start(f32[1024,32,64]{0,2,1:T(8,128)} %reshape_squeeze.7) | copy-start | bytes 25165828
  1320.7 17.4 %copy-start.5 = (f32[32,64]{0,1:T(8,128)S(1)}, f32[32,64]{0,1:T(8,128)}, u32[]{:S(2)}) copy-start(f32[32,64]{0,1:T(8,128)} %copy-done.4) | copy-start | bytes 24580
  1320.7 17.4 %copy-start.7 = (f32[32,64]{0,1:T(8,128)S(1)}, f32[32,64]{0,1:T(8,128)}, u32[]{:S(2)}) copy-start(f32[32,64]{0,1:T(8,128)} %copy-done.6) | copy-start | bytes 24580
  1362.3 15.9 %copy-start.1 = (f32[1024,32,64]{0,1,2:T(8,128)S(1)}, f32[1024,32,64]{0,1,2:T(8,128)}, u32[]{:S(2)}) copy-start(f32[1024,32,64]{0,1,2:T(8,128)} %get-tuple-element.11) | copy-start | bytes 25165828
  1362.3 29.7 %slice-start = ((s8[8388608]{0:T(1024)(128)(4,1)}), s8[4194304]{0:T(1024)(128)(4,1)S(1)}, s32[]{:S(2)}) async-start(s8[8388608]{0:T(1024)(128)(4,1)} %bitcast.117), calls=%async_computation.5 | async-start | bytes 8388608
  1378.3 13.7 slice-start.1
where the time goes:
time: 1500 us; the launch traced here: 1490 us
  blocking collectives  743 us (50%)
  local copies, waits for them, and re-layouts  283 us (19%)
  waiting for transfers between devices  225 us (15%)
  matrix products  222 us (15%)
    all_to_all x1, blocking collectives, body(): lax.all_to_all(lax.all_to_all(sectioned, 'row', split_axis=1, concat_axis...  368 us
    dot_general x14, matrix products, mixed(): return jnp.einsum(form, left, right, precision=lax.Precision.HIGHEST)  199 us
    all_to_all x1, blocking collectives, body(): lax.all_to_all(outgoing, 'col', split_axis=0, concat_axis=0, tiled=True)  190 us
    all_to_all x1, blocking collectives, body(): lax.all_to_all(sectioned, 'row', split_axis=1, concat_axis=1, tiled=True)  185 us
    all_to_all x1, waiting for transfers between devices, body(): lax.all_to_all(pencil_input, 'col', split_axis=1, concat_axis=4, tiled=True)  166 us
    all_to_all x1, waiting for transfers between devices, body(): lax.all_to_all(lax.all_to_all(outgoing, 'col', split_axis=0, concat_axis=...  58.5 us
    slice x3, local copies, waits for them, and re-layouts, body(): final_re, final_im = spectral(spectra[0], spectra[1])  35.4 us
    unnamed x23, local copies, waits for them, and re-layouts  34.7 us
  transfers between devices with their start and end apart: 2, of which 2 were waited for; matrix products, arithmetic and copies ran while one was open for 3% of the time, Pallas kernels for 0%

commit v1 on v0

--- a/solution.py
+++ b/solution.py
@@ -3,6 +3,8 @@
 import jax
 import jax.numpy as jnp
 from jax import lax
+from jax.experimental import pallas as pl
+from jax.experimental.pallas import tpu as pltpu
 from jax.sharding import PartitionSpec as P
 
 N = 2048
@@ -98,7 +100,7 @@
     return (distance.astype(jnp.float32) >= radius).astype(jnp.float32)
 
 
-def body(intensity, punch_radius):
+def pencil_body(intensity, punch_radius):
     row_count = lax.axis_size("row")
     col_count = lax.axis_size("col")
     row_at = lax.axis_index("row")
@@ -159,6 +161,241 @@
     return (out_re, out_im)
 
 
+RADIX = 4
+
+
+def spin(first_ids, second_ids, period):
+    phases = first_ids * second_ids % period
+    angles = phases.astype(jnp.float32) * (2.0 * math.pi / period)
+    return jnp.cos(angles), jnp.sin(angles)
+
+
+def halves(values):
+    high = lax.reduce_precision(values, exponent_bits=8, mantissa_bits=7)
+    return high.astype(jnp.bfloat16), (values - high).astype(jnp.bfloat16)
+
+
+def packed(coarse, fine, shape):
+    coarse_re, coarse_im = coarse
+    fine_re, fine_im = fine
+    full_re = (coarse_re * fine_re - coarse_im * fine_im).reshape(shape)
+    full_im = (coarse_re * fine_im + coarse_im * fine_re).reshape(shape)
+    return jnp.stack([*halves(full_re), *halves(full_im)])
+
+
+def twiddles(length):
+    width = length // RADIX
+    fine = 16
+    ids = jnp.arange(width, dtype=jnp.int32)
+    lead = jnp.arange(RADIX, dtype=jnp.int32)[:, None, None, None]
+    high_ids = (jnp.arange(width // fine, dtype=jnp.int32) * fine)[None, :, None, None]
+    low_ids = jnp.arange(fine, dtype=jnp.int32)[None, None, :, None]
+    minor = ids[None, None, None, :]
+    shape = (RADIX, width, width)
+    sample = RADIX * minor + lead
+    freq_major = packed(spin(sample, high_ids, length), spin(sample, low_ids, length), shape)
+    time_major = packed(
+        spin(RADIX * high_ids, minor, length), spin(RADIX * low_ids + lead, minor, length), shape
+    )
+    return freq_major, time_major
+
+
+def dot32(left, right):
+    return jnp.dot(left, right, preferred_element_type=jnp.float32)
+
+
+def symmetrize(direct_ref, mirror_ref, near_ref, far_ref, pick_ref, order_ref, flip_ref, sym_ref):
+    groups, _, block, width = direct_ref.shape
+    rows = lax.broadcasted_iota(jnp.int32, (block, width), 0)
+    cols = lax.broadcasted_iota(jnp.int32, (block, width), 1)
+    row_off = (rows + SP // 2) % SP - SP // 2
+    col_off = (cols + SP // 2) % SP - SP // 2
+    distance = (row_off * row_off + col_off * col_off).astype(jnp.float32)
+    merged = []
+    for part in range(groups):
+        picked = pick_ref[:, part * width : (part + 1) * width]
+        keep_mirror = distance >= dot32(near_ref[0], picked)
+        keep_direct = distance >= dot32(far_ref[0], picked)
+        turned = jnp.concatenate(
+            [
+                direct_ref[piece, 0, part * width : (part + 1) * width, :].T
+                for piece in range(groups)
+            ],
+            axis=0,
+        )
+        total = jnp.where(keep_mirror, mirror_ref[0, part, 0], 0.0) + jnp.where(
+            keep_direct, turned, 0.0
+        )
+        scale = jnp.where(keep_mirror & keep_direct, 0.5, 1.0)
+        merged.append((total * scale).astype(jnp.bfloat16))
+    sym = jnp.concatenate(merged, axis=1)
+    sorted_rows = dot32(order_ref[...], sym).astype(jnp.bfloat16)
+    sorted_both = dot32(sorted_rows, flip_ref[...]).astype(jnp.bfloat16)
+    sym_ref[0] = sorted_both.reshape(sym_ref.shape[1:])
+
+
+def butterfly(res, ims):
+    even_re, odd_re = res[0] + res[2], res[0] - res[2]
+    even_im, odd_im = ims[0] + ims[2], ims[0] - ims[2]
+    pair_re, gap_re = res[1] + res[3], res[1] - res[3]
+    pair_im, gap_im = ims[1] + ims[3], ims[1] - ims[3]
+    out_re = (even_re + pair_re, odd_re - gap_im, even_re - pair_re, odd_re + gap_im)
+    out_im = (even_im + pair_im, odd_im + gap_re, even_im - pair_im, odd_im - gap_re)
+    return out_re, out_im
+
+
+def transform_first(table_ref, sym_ref, part_ref):
+    res, ims = [], []
+    for lead in range(RADIX):
+        data = sym_ref[0, lead]
+        res.append(dot32(table_ref[0, lead], data) + dot32(table_ref[1, lead], data))
+        ims.append(dot32(table_ref[2, lead], data) + dot32(table_ref[3, lead], data))
+    out_re, out_im = butterfly(res, ims)
+    for block in range(RADIX):
+        part_ref[block, 0, 0] = out_re[block].astype(part_ref.dtype)
+        part_ref[block, 1, 0] = out_im[block].astype(part_ref.dtype)
+
+
+def transform_second(scale, part_ref, table_ref, out_ref):
+    sources, _, _, _, width = part_ref.shape
+    piece = width // RADIX
+    res, ims = [], []
+    for lead in range(RADIX):
+        data_re, data_im = (
+            jnp.concatenate(
+                [
+                    part_ref[source, which, 0, :, lead * piece : (lead + 1) * piece]
+                    for source in range(sources)
+                ],
+                axis=1,
+            )
+            for which in range(2)
+        )
+        res.append(
+            dot32(data_re, table_ref[0, lead])
+            + dot32(data_re, table_ref[1, lead])
+            - dot32(data_im, table_ref[2, lead])
+            - dot32(data_im, table_ref[3, lead])
+        )
+        ims.append(
+            dot32(data_re, table_ref[2, lead])
+            + dot32(data_re, table_ref[3, lead])
+            + dot32(data_im, table_ref[0, lead])
+            + dot32(data_im, table_ref[1, lead])
+        )
+    out_re, out_im = butterfly(res, ims)
+    owners, _, _, rows, _ = out_ref.shape
+    for which, values in ((0, out_re), (1, out_im)):
+        for block in range(RADIX):
+            ready = (values[block] * scale).astype(out_ref.dtype)
+            span = ready.shape[1]
+            for owner in range(owners):
+                out_ref[owner, which, 0, :, block * span : (block + 1) * span] = ready[
+                    owner * rows : (owner + 1) * rows
+                ]
+
+
+LIMIT = 56 * 1024 * 1024
+
+
+def plane_body(intensity, punch_radius):
+    row_count = lax.axis_size("row")
+    col_count = lax.axis_size("col")
+    row_at = lax.axis_index("row")
+    col_at = lax.axis_index("col")
+    planes, h_block, k_block = intensity.shape
+    held = planes // col_count
+    groups = h_block // k_block
+    length = h_block * row_count
+    width = length // RADIX
+    piece = h_block // RADIX
+    freq_width = length // (row_count * col_count)
+    bf16 = jnp.bfloat16
+
+    direct = lax.all_to_all(intensity, "col", split_axis=0, concat_axis=0, tiled=True)
+    mirror = lax.all_to_all(direct, "row", split_axis=0, concat_axis=0, tiled=True)
+    direct = direct.reshape(col_count, held, h_block, k_block)
+    mirror = mirror.reshape(row_count, groups, held, h_block, k_block)
+
+    levels = held * col_at + jnp.arange(held, dtype=jnp.int32)
+    plane_node = (levels + SP // 2) // SP
+    plane_off = levels - SP * plane_node
+    level_ids = jnp.arange(punch_radius.shape[0], dtype=jnp.int32)
+    chosen = (plane_node[:, None] == level_ids[None, :]).astype(jnp.int32)
+    table = jnp.sum(chosen[:, :, None, None] * punch_radius[None], axis=1)
+    table = (table - (plane_off * plane_off)[:, None, None]).astype(bf16)
+    node_count = punch_radius.shape[1]
+    node_ids = jnp.arange(node_count, dtype=jnp.int32)
+    whole = jnp.arange(length, dtype=jnp.int32)
+    pick_k = ((whole[:, None] + SP // 2) // SP == node_ids[None, :]).astype(bf16)
+    mine = h_block * row_at + jnp.arange(h_block, dtype=jnp.int32)
+    pick_h = ((mine[None, :] + SP // 2) // SP == node_ids[:, None]).astype(bf16)
+    near = jnp.einsum("kn,lnm->lkm", pick_k, table, preferred_element_type=jnp.float32)
+    far = jnp.einsum("kn,lmn->lkm", pick_k, table, preferred_element_type=jnp.float32)
+    near, far = near.astype(bf16), far.astype(bf16)
+    local = jnp.arange(h_block, dtype=jnp.int32)
+    source = RADIX * (local % piece) + local // piece
+    order = (source[:, None] == local[None, :]).astype(bf16)
+    flip = (source[None, :] == local[:, None]).astype(bf16)
+    freq_major, time_major = twiddles(length)
+
+    sym = pl.pallas_call(
+        symmetrize,
+        out_shape=jax.ShapeDtypeStruct((held, RADIX, width, h_block), bf16),
+        grid=(held, row_count),
+        in_specs=[
+            pl.BlockSpec((groups, 1, h_block, k_block), lambda p, r: (r, p, 0, 0)),
+            pl.BlockSpec((1, groups, 1, h_block, k_block), lambda p, r: (r, 0, p, 0, 0)),
+            pl.BlockSpec((1, h_block, node_count), lambda p, r: (p, r, 0)),
+            pl.BlockSpec((1, h_block, node_count), lambda p, r: (p, r, 0)),
+            pl.BlockSpec((node_count, h_block), lambda p, r: (0, 0)),
+            pl.BlockSpec((h_block, h_block), lambda p, r: (0, 0)),
+            pl.BlockSpec((h_block, h_block), lambda p, r: (0, 0)),
+        ],
+        out_specs=pl.BlockSpec((1, RADIX, piece, h_block), lambda p, r: (p, 0, r, 0)),
+        compiler_params=pltpu.CompilerParams(vmem_limit_bytes=LIMIT),
+    )(direct, mirror, near, far, pick_h, order, flip)
+
+    tile = min(128, width)
+    parts = pl.pallas_call(
+        transform_first,
+        out_shape=jax.ShapeDtypeStruct((RADIX, 2, held, width, h_block), bf16),
+        grid=(width // tile, held),
+        in_specs=[
+            pl.BlockSpec((4, RADIX, tile, width), lambda d, p: (0, 0, d, 0)),
+            pl.BlockSpec((1, RADIX, width, h_block), lambda d, p: (p, 0, 0, 0)),
+        ],
+        out_specs=pl.BlockSpec((RADIX, 2, 1, tile, h_block), lambda d, p: (0, 0, p, d, 0)),
+        compiler_params=pltpu.CompilerParams(vmem_limit_bytes=LIMIT),
+    )(freq_major, sym)
+
+    parts = lax.all_to_all(parts, "row", split_axis=0, concat_axis=0, tiled=True)
+
+    owners = max(1, tile // freq_width)
+    rows = owners * freq_width
+    spectra = pl.pallas_call(
+        lambda *refs: transform_second(1.0 / length, *refs),
+        out_shape=jax.ShapeDtypeStruct((col_count, 2, held, freq_width, length), bf16),
+        grid=(held, width // rows),
+        in_specs=[
+            pl.BlockSpec((row_count, 2, 1, rows, h_block), lambda p, d: (0, 0, p, d, 0)),
+            pl.BlockSpec((4, RADIX, width, width), lambda p, d: (0, 0, 0, 0)),
+        ],
+        out_specs=pl.BlockSpec((owners, 2, 1, freq_width, length), lambda p, d: (d, 0, p, 0, 0)),
+        compiler_params=pltpu.CompilerParams(vmem_limit_bytes=LIMIT),
+    )(parts, time_major)
+
+    spectra = lax.all_to_all(spectra, "col", split_axis=0, concat_axis=0, tiled=True)
+    out_re = spectra[:, 0].reshape(planes, freq_width, length).astype(jnp.float32)
+    out_im = spectra[:, 1].reshape(planes, freq_width, length).astype(jnp.float32)
+    return out_re, out_im
+
+
+def body(intensity, punch_radius):
+    by_plane = lax.axis_size("row") == RADIX and intensity.shape[0] % lax.axis_size("col") == 0
+    return (plane_body if by_plane else pencil_body)(intensity, punch_radius)
+
+
 def solution(mesh):
     in_specs = (P(None, "row", "col"), P())
     out_specs = (P(None, ("row", "col"), None), P(None, ("row", "col"), None))

time: 1500 us -> 644 us (0.43)
  blocking collectives: 743 us -> 378 us
  local copies, waits for them, and re-layouts: 283 us -> 7.25 us
  matrix products: 222 us -> 1.1 us
  waiting for transfers between devices: 225 us -> 159 us
  Pallas kernels: 0 us -> 58.3 us
  other arithmetic: 5.38 us -> 27.7 us
    all_to_all x3 -> x2, blocking collectives: 743 us -> 378 us  [the longest x1 190 us: plane_body(): lax.all_to_all(intensity, 'col', split_axis=0, concat_axis=0, tiled=True)]
    dot_general x18 -> x2, matrix products: 222 us -> 1.1 us  [the longest x1 0.59 us: plane_body(): jnp.einsum('kn,lnm->lkm', pick_k, table, preferred_element_type=jnp.float32)]
    all_to_all x2, waiting for transfers between devices: 225 us -> 159 us  [the longest x1 83.4 us: plane_body(): lax.all_to_all(parts, 'row', split_axis=0, concat_axis=0, tiled=True)]
    pallas_call x0 -> x3, Pallas kernels: none -> 58.3 us  [the longest x1 24.9 us: plane_body(): pl.pallas_call(lambda *refs: transform_second(1.0 / length, *refs), out_s...]
    all_to_all x4 -> x0, local copies, waits for them, and re-layouts: 52.1 us -> none  [the longest x1 22.9 us: body(): lax.all_to_all(lax.all_to_all(sectioned, 'row', split_axis=1, concat_axis...]
    div x4 -> x0, local copies, waits for them, and re-layouts: 46.4 us -> none  [the longest x2 24.8 us: body(): out_im = (final_im / N).reshape(planes, freq_width, N)]
    reshape x4 -> x0, local copies, waits for them, and re-layouts: 45.4 us -> none  [the longest x2 24.8 us: spectral_lead(): grid_re = real_in.reshape(row_total, first, second)]
    unnamed x23 -> x2, local copies, waits for them, and re-layouts: 34.7 us -> 0.01 us
  transfers between devices with their start and end apart: 2 -> 2, of which waited for: 2 -> 2; matrix products, arithmetic and copies ran while one was open for 3% -> 4% of each run, Pallas kernels for 0% -> 0%
where the time goes in v1:
time: 644 us
  blocking collectives  378 us (59%)
  waiting for transfers between devices  159 us (25%)
  Pallas kernels  58.3 us (9%)
  other arithmetic  27.7 us (4%)
  starting transfers between devices  11.6 us (2%)
  local copies, waits for them, and re-layouts  7.25 us (1%)
    all_to_all x1, blocking collectives, plane_body(): lax.all_to_all(intensity, 'col', split_axis=0, concat_axis=0, tiled=True)  190 us
    all_to_all x1, blocking collectives, plane_body(): lax.all_to_all(spectra, 'col', split_axis=0, concat_axis=0, tiled=True)  188 us
    all_to_all x1, waiting for transfers between devices, plane_body(): lax.all_to_all(parts, 'row', split_axis=0, concat_axis=0, tiled=True)  83.4 us
    all_to_all x1, waiting for transfers between devices, plane_body(): lax.all_to_all(direct, 'row', split_axis=0, concat_axis=0, tiled=True)  75.4 us
    pallas_call x1, Pallas kernels, plane_body(): pl.pallas_call(lambda *refs: transform_second(1.0 / length, *refs), out_s...  24.9 us
    pallas_call x1, Pallas kernels, plane_body(): pl.pallas_call(transform_first, out_shape=jax.ShapeDtypeStruct((RADIX, 2,...  18.9 us
    pallas_call x1, Pallas kernels, plane_body(): pl.pallas_call(symmetrize, out_shape=jax.ShapeDtypeStruct((held, RADIX, w...  14.5 us
  transfers between devices with their start and end apart: 2, of which 2 were waited for; matrix products, arithmetic and copies ran while one was open for 4% of the time, Pallas kernels for 0%

profile of v1, /device:TPU:0, one launch (start us, length us, event | category | flops | bytes accessed | tf_op | source)
XLA Modules:
  0.0 643.6 jit_solution(11331160094568011291)
XLA Ops:
  0.6 190.5 %all_to_all.20 = f32[16,512,256]{2,1,0:T(8,128)} all-to-all(f32[16,512,256]{2,1,0:T(8,128)} %param.2), channel_id=1, replica_groups=mesh['row'=4,'col'=8] {'col'}, dimensions={0} | all-to-all | bytes 16777216 | tf_op jit(solution)/shard_map/all_to_all | solution.py:315
  191.1 0.0 copy-start
  191.1 5.8 all-to-all-start.1
  196.9 0.1 compare_convert_fusion
  197.0 0.0 copy-done
  197.0 0.7 multiply_reduce_fusion
  197.7 0.6 convolution_convert_fusion.1
  198.3 2.4 copy.13
  200.7 0.5 convolution_convert_fusion
  201.2 2.4 copy.15
  203.6 0.7 fusion.11.pick_ref
  204.3 0.5 fusion.37
  204.9 1.1 fusion.26
  206.0 1.2 fusion.8
  207.1 1.3 multiply_subtract_fusion.1
  208.5 1.7 reduce-precision_convert_fusion.2
  210.2 3.9 pad_maximum_fusion.table_ref
  214.0 75.4 %all-to-all-done.1 = f32[16,512,256]{2,1,0:T(8,128)} async-done(((f32[16,512,256]{2,1,0:T(8,128)}), f32[16,512,256]{2,1,0:T(8,128)}, u32[]{:S(2)}, u32[]{:S(2)}) %all-to-all-start.1) | async-done | bytes 8388640 | tf_op jit(solution)/shard_map/all_to_all | solution.py:316
  289.5 14.5 %shard_map.41.sym_ref = bf16[2,4,512,512]{3,2,1,0:T(8,128)(2,1)} custom-call(f32[8,2,512,256]{3,2,1,0:T(8,128)} %bitcast.20, f32[4,2,2,512,256]{4,3,2,1,0:T(8,128)} %bitcast.3.mirror_ref, bf16[2,2048,129]{2,1,0:T(8,128)(2,1)} %bitcast.25, bf16[2,2048,129]{2,1,0:T(8,128)(2,1)} %bitcast.26, bf16[129,512]{1,0:T(8,128)(2,1)} %fusion.11.pick_ref, ...), custom_call_target="tpu_custom_call" | custom-call | tf_op jit(solution)/shard_map/pallas_call | solution.py:342
  304.0 18.9 %shard_map.42 = bf16[4,2,2,512,512]{4,3,2,1,0:T(8,128)(2,1)} custom-call(bf16[4,4,512,512]{3,2,1,0:T(8,128)(2,1)} %pad_maximum_fusion.table_ref, bf16[2,4,512,512]{3,2,1,0:T(8,128)(2,1)} %shard_map.41.sym_ref), custom_call_target="tpu_custom_call" | custom-call | tf_op jit(solution)/shard_map/pallas_call | solution.py:360
  322.9 5.8 all-to-all-start.2
  328.7 0.3 fusion.40
  329.0 0.6 fusion.34
  329.6 0.1 mul.670
  329.8 0.1 mul.681
  329.9 0.5 mul.684
  330.4 0.5 mul.678
  331.0 2.1 reduce-precision_convert_fusion.1
  333.1 3.9 pad_maximum_fusion.1.refs_1_
  337.0 83.4 %all-to-all-done.2.refs_0_ = bf16[4,2,2,512,512]{4,3,2,1,0:T(8,128)(2,1)} async-done(((bf16[4,2,2,512,512]{4,3,2,1,0:T(8,128)(2,1)}), bf16[4,2,2,512,512]{4,3,2,1,0:T(8,128)(2,1)}, u32[]{:S(2)}, u32[]{:S(2)}) %all-to-all-start.2) | async-done | bytes 8388640 | tf_op jit(solution)/shard_map/all_to_all | solution.py:372
  420.4 24.9 %shard_map.43 = bf16[8,2,2,64,2048]{4,3,2,1,0:T(8,128)(2,1)} custom-call(bf16[4,2,2,512,512]{4,3,2,1,0:T(8,128)(2,1)} %all-to-all-done.2.refs_0_, bf16[4,4,512,512]{3,2,1,0:T(8,128)(2,1)} %pad_maximum_fusion.1.refs_1_), custom_call_target="tpu_custom_call" | custom-call | tf_op jit(solution)/shard_map/pallas_call | solution.py:376
  445.3 187.6 %all_to_all.21 = bf16[8,2,2,64,2048]{4,3,2,1,0:T(8,128)(2,1)S(1)} all-to-all(bf16[8,2,2,64,2048]{4,3,2,1,0:T(8,128)(2,1)} %shard_map.43), channel_id=1, replica_groups=mesh['row'=4,'col'=8] {'col'}, dimensions={0} | all-to-all | bytes 16777216 | tf_op jit(solution)/shard_map/all_to_all | solution.py:388
  632.9 1.2 fusion.56
  634.1 4.7 bitcast_convert_fusion
  638.9 4.7 bitcast_convert_fusion.1
  (10 shorter events, 0.1 us)
Async XLA Ops:
  191.1 5.9 copy-start
  191.1 98.4 %all-to-all-start.1 = ((f32[16,512,256]{2,1,0:T(8,128)}), f32[16,512,256]{2,1,0:T(8,128)}, u32[]{:S(2)}, u32[]{:S(2)}) async-start(f32[16,512,256]{2,1,0:T(8,128)} %all_to_all.20), calls=%async_computation.1 | async-start | bytes 16777216 | tf_op jit(solution)/shard_map/all_to_all | solution.py:316
  322.9 97.5 %all-to-all-start.2 = ((bf16[4,2,2,512,512]{4,3,2,1,0:T(8,128)(2,1)}), bf16[4,2,2,512,512]{4,3,2,1,0:T(8,128)(2,1)}, u32[]{:S(2)}, u32[]{:S(2)}) async-start(bf16[4,2,2,512,512]{4,3,2,1,0:T(8,128)(2,1)} %shard_map.42), calls=%async_computation.2 | async-start | bytes 16777216 | tf_op jit(solution)/shard_map/all_to_all | solution.py:372

commit v2 on v1

--- a/solution.py
+++ b/solution.py
@@ -295,6 +295,79 @@
                 ]
 
 
+def swap_kernel(send_ref, got_ref, stage, send_sem, recv_sem, local_sem):
+    count = send_ref.shape[0]
+    me = lax.axis_index("row")
+    barrier = pltpu.get_barrier_semaphore()
+    for step in range(1, count):
+        pl.semaphore_signal(barrier, inc=1, device_id={"row": lax.rem(me + step, count)})
+    pl.semaphore_wait(barrier, count - 1)
+    copies = []
+    for step in range(1, count):
+        peer = lax.rem(me + step, count)
+        copy = pltpu.make_async_remote_copy(
+            src_ref=send_ref.at[peer],
+            dst_ref=got_ref.at[me],
+            send_sem=send_sem.at[step - 1],
+            recv_sem=recv_sem.at[step - 1],
+            device_id={"row": peer},
+        )
+        copy.start()
+        copies.append(copy)
+    load = pltpu.make_async_copy(send_ref.at[me], stage, local_sem.at[0])
+    load.start()
+    load.wait()
+    store = pltpu.make_async_copy(stage, got_ref.at[me], local_sem.at[1])
+    store.start()
+    store.wait()
+    for copy in copies:
+        copy.wait()
+
+
+def swap(values, identity):
+    count = values.shape[0]
+    return pl.pallas_call(
+        swap_kernel,
+        out_shape=jax.ShapeDtypeStruct(values.shape, values.dtype),
+        in_specs=[pl.BlockSpec(memory_space=pl.ANY)],
+        out_specs=pl.BlockSpec(memory_space=pl.ANY),
+        scratch_shapes=[
+            pltpu.VMEM(values.shape[1:], values.dtype),
+            pltpu.SemaphoreType.DMA((count - 1,)),
+            pltpu.SemaphoreType.DMA((count - 1,)),
+            pltpu.SemaphoreType.DMA((2,)),
+        ],
+        compiler_params=pltpu.CompilerParams(collective_id=identity, has_side_effects=True),
+        cost_estimate=pl.CostEstimate(
+            flops=40 * 10**9, bytes_accessed=values.size * 4, transcendentals=0
+        ),
+    )(values)
+
+
+def widen_kernel(got_ref, *refs):
+    re_ref, im_ref = refs[-2:]
+    re_ref[0, 0] = got_ref[0, 0, 0].astype(jnp.float32)
+    im_ref[0, 0] = got_ref[0, 1, 0].astype(jnp.float32)
+
+
+def widen(at, held, received, outs):
+    owners, _, _, rows, length = received.shape
+    shape = jax.ShapeDtypeStruct((owners, held, rows, length), jnp.float32)
+    spec = pl.BlockSpec((1, 1, rows, length), lambda c: (c, at, 0, 0))
+    return pl.pallas_call(
+        widen_kernel,
+        out_shape=(shape, shape),
+        grid=(owners,),
+        in_specs=[pl.BlockSpec((1, 2, 1, rows, length), lambda c: (c, 0, 0, 0, 0))]
+        + [pl.BlockSpec(memory_space=pl.ANY)] * len(outs),
+        out_specs=(spec, spec),
+        input_output_aliases={1 + which: which for which in range(len(outs))},
+        cost_estimate=pl.CostEstimate(
+            flops=8 * 10**9, bytes_accessed=received.size * 6, transcendentals=0
+        ),
+    )(received, *outs)
+
+
 LIMIT = 56 * 1024 * 1024
 
 
@@ -311,11 +384,6 @@
     piece = h_block // RADIX
     freq_width = length // (row_count * col_count)
     bf16 = jnp.bfloat16
-
-    direct = lax.all_to_all(intensity, "col", split_axis=0, concat_axis=0, tiled=True)
-    mirror = lax.all_to_all(direct, "row", split_axis=0, concat_axis=0, tiled=True)
-    direct = direct.reshape(col_count, held, h_block, k_block)
-    mirror = mirror.reshape(row_count, groups, held, h_block, k_block)
 
     levels = held * col_at + jnp.arange(held, dtype=jnp.int32)
     plane_node = (levels + SP // 2) // SP
@@ -339,56 +407,89 @@
     flip = (source[None, :] == local[:, None]).astype(bf16)
     freq_major, time_major = twiddles(length)
 
-    sym = pl.pallas_call(
-        symmetrize,
-        out_shape=jax.ShapeDtypeStruct((held, RADIX, width, h_block), bf16),
-        grid=(held, row_count),
-        in_specs=[
-            pl.BlockSpec((groups, 1, h_block, k_block), lambda p, r: (r, p, 0, 0)),
-            pl.BlockSpec((1, groups, 1, h_block, k_block), lambda p, r: (r, 0, p, 0, 0)),
-            pl.BlockSpec((1, h_block, node_count), lambda p, r: (p, r, 0)),
-            pl.BlockSpec((1, h_block, node_count), lambda p, r: (p, r, 0)),
-            pl.BlockSpec((node_count, h_block), lambda p, r: (0, 0)),
-            pl.BlockSpec((h_block, h_block), lambda p, r: (0, 0)),
-            pl.BlockSpec((h_block, h_block), lambda p, r: (0, 0)),
-        ],
-        out_specs=pl.BlockSpec((1, RADIX, piece, h_block), lambda p, r: (p, 0, r, 0)),
-        compiler_params=pltpu.CompilerParams(vmem_limit_bytes=LIMIT),
-    )(direct, mirror, near, far, pick_h, order, flip)
-
     tile = min(128, width)
-    parts = pl.pallas_call(
-        transform_first,
-        out_shape=jax.ShapeDtypeStruct((RADIX, 2, held, width, h_block), bf16),
-        grid=(width // tile, held),
-        in_specs=[
-            pl.BlockSpec((4, RADIX, tile, width), lambda d, p: (0, 0, d, 0)),
-            pl.BlockSpec((1, RADIX, width, h_block), lambda d, p: (p, 0, 0, 0)),
-        ],
-        out_specs=pl.BlockSpec((RADIX, 2, 1, tile, h_block), lambda d, p: (0, 0, p, d, 0)),
-        compiler_params=pltpu.CompilerParams(vmem_limit_bytes=LIMIT),
-    )(freq_major, sym)
-
-    parts = lax.all_to_all(parts, "row", split_axis=0, concat_axis=0, tiled=True)
-
     owners = max(1, tile // freq_width)
     rows = owners * freq_width
-    spectra = pl.pallas_call(
-        lambda *refs: transform_second(1.0 / length, *refs),
-        out_shape=jax.ShapeDtypeStruct((col_count, 2, held, freq_width, length), bf16),
-        grid=(held, width // rows),
-        in_specs=[
-            pl.BlockSpec((row_count, 2, 1, rows, h_block), lambda p, d: (0, 0, p, d, 0)),
-            pl.BlockSpec((4, RADIX, width, width), lambda p, d: (0, 0, 0, 0)),
-        ],
-        out_specs=pl.BlockSpec((owners, 2, 1, freq_width, length), lambda p, d: (d, 0, p, 0, 0)),
-        compiler_params=pltpu.CompilerParams(vmem_limit_bytes=LIMIT),
-    )(parts, time_major)
-
-    spectra = lax.all_to_all(spectra, "col", split_axis=0, concat_axis=0, tiled=True)
-    out_re = spectra[:, 0].reshape(planes, freq_width, length).astype(jnp.float32)
-    out_im = spectra[:, 1].reshape(planes, freq_width, length).astype(jnp.float32)
-    return out_re, out_im
+    params = pltpu.CompilerParams(vmem_limit_bytes=LIMIT)
+    split = intensity.reshape(col_count, held, h_block, k_block)
+
+    def gather(at):
+        return lax.all_to_all(split[:, at], "col", split_axis=0, concat_axis=0, tiled=True)
+
+    def first(at, direct, mirror):
+        sym = pl.pallas_call(
+            symmetrize,
+            out_shape=jax.ShapeDtypeStruct((1, RADIX, width, h_block), bf16),
+            grid=(1, row_count),
+            in_specs=[
+                pl.BlockSpec((groups, 1, h_block, k_block), lambda p, r: (r, p, 0, 0)),
+                pl.BlockSpec((1, groups, 1, h_block, k_block), lambda p, r: (r, 0, p, 0, 0)),
+                pl.BlockSpec((1, h_block, node_count), lambda p, r: (p, r, 0)),
+                pl.BlockSpec((1, h_block, node_count), lambda p, r: (p, r, 0)),
+                pl.BlockSpec((node_count, h_block), lambda p, r: (0, 0)),
+                pl.BlockSpec((h_block, h_block), lambda p, r: (0, 0)),
+                pl.BlockSpec((h_block, h_block), lambda p, r: (0, 0)),
+            ],
+            out_specs=pl.BlockSpec((1, RADIX, piece, h_block), lambda p, r: (p, 0, r, 0)),
+            compiler_params=params,
+            cost_estimate=pl.CostEstimate(
+                flops=14 * 10**9, bytes_accessed=10**7, transcendentals=0
+            ),
+        )(
+            direct.reshape(col_count, 1, h_block, k_block),
+            mirror.reshape(row_count, groups, 1, h_block, k_block),
+            near[at : at + 1],
+            far[at : at + 1],
+            pick_h,
+            order,
+            flip,
+        )
+        return pl.pallas_call(
+            transform_first,
+            out_shape=jax.ShapeDtypeStruct((RADIX, 2, 1, width, h_block), bf16),
+            grid=(width // tile, 1),
+            in_specs=[
+                pl.BlockSpec((4, RADIX, tile, width), lambda d, p: (0, 0, d, 0)),
+                pl.BlockSpec((1, RADIX, width, h_block), lambda d, p: (p, 0, 0, 0)),
+            ],
+            out_specs=pl.BlockSpec((RADIX, 2, 1, tile, h_block), lambda d, p: (0, 0, p, d, 0)),
+            compiler_params=params,
+            cost_estimate=pl.CostEstimate(
+                flops=14 * 10**9, bytes_accessed=10**7, transcendentals=0
+            ),
+        )(freq_major, sym)
+
+    def second(parts):
+        return pl.pallas_call(
+            lambda *refs: transform_second(1.0 / length, *refs),
+            out_shape=jax.ShapeDtypeStruct((col_count, 2, 1, freq_width, length), bf16),
+            grid=(1, width // rows),
+            in_specs=[
+                pl.BlockSpec((row_count, 2, 1, rows, h_block), lambda p, d: (0, 0, p, d, 0)),
+                pl.BlockSpec((4, RADIX, width, width), lambda p, d: (0, 0, 0, 0)),
+            ],
+            out_specs=pl.BlockSpec(
+                (owners, 2, 1, freq_width, length), lambda p, d: (d, 0, p, 0, 0)
+            ),
+            compiler_params=params,
+            cost_estimate=pl.CostEstimate(
+                flops=14 * 10**9, bytes_accessed=10**7, transcendentals=0
+            ),
+        )(parts, time_major)
+
+    directs = [gather(at) for at in range(held)]
+    mirrors = [
+        swap(direct.reshape(row_count, groups, h_block, k_block), 0) for direct in directs
+    ]
+    parts = [swap(first(at, directs[at], mirrors[at]), 1) for at in range(held)]
+    spectra = [
+        lax.all_to_all(second(part), "col", split_axis=0, concat_axis=0, tiled=True)
+        for part in parts
+    ]
+    outs = ()
+    for at, received in enumerate(spectra):
+        outs = widen(at, held, received, outs)
+    return tuple(half.reshape(planes, freq_width, length) for half in outs)
 
 
 def body(intensity, punch_radius):

time: 644 us -> 543 us (0.84)
  blocking collectives: 378 us -> 0 us
  Pallas kernels: 58.3 us -> 274 us
  waiting for transfers between devices: 159 us -> 204 us
  starting transfers between devices: 11.6 us -> 20.6 us
  local copies, waits for them, and re-layouts: 7.25 us -> 16.2 us
    all_to_all x2 -> x0, blocking collectives: 378 us -> none  [the longest x1 190 us: plane_body(): lax.all_to_all(intensity, 'col', split_axis=0, concat_axis=0, tiled=True)]
    pallas_call x3 -> x12, Pallas kernels: 58.3 us -> 274 us  [the longest x4 195 us: swap(): pl.pallas_call(swap_kernel, out_shape=jax.ShapeDtypeStruct(values.shape,...]
    all_to_all x2 -> x4, waiting for transfers between devices: 159 us -> 204 us  [the longest x2 104 us: gather(): lax.all_to_all(split[:, at], 'col', split_axis=0, concat_axis=0, tiled=True)]
    convert_element_type x2 -> x0, other arithmetic: 9.49 us -> none  [the longest x1 4.75 us: plane_body(): spectra[:, 1].reshape(planes, freq_width, length).astype(jnp.float32)]
    all_to_all x2 -> x4, starting transfers between devices: 11.6 us -> 20.6 us  [the longest x2 11.3 us: gather(): lax.all_to_all(split[:, at], 'col', split_axis=0, concat_axis=0, tiled=True)]
    squeeze x0 -> x1, local copies, waits for them, and re-layouts: none -> 7.49 us  [gather(): split[:, at]]
  transfers between devices with their start and end apart: 2 -> 4, of which waited for: 2 -> 4; matrix products, arithmetic and copies ran while one was open for 4% -> 6% of each run, Pallas kernels for 0% -> 25%
where the time goes in v2:
time: 543 us; the launch traced here: 542 us
  Pallas kernels  274 us (50%)
  waiting for transfers between devices  204 us (38%)
  other arithmetic  24.7 us (5%)
  starting transfers between devices  20.6 us (4%)
  local copies, waits for them, and re-layouts  16.2 us (3%)
    pallas_call x4, Pallas kernels, swap(): pl.pallas_call(swap_kernel, out_shape=jax.ShapeDtypeStruct(values.shape,...  195 us
    all_to_all x2, waiting for transfers between devices, gather(): lax.all_to_all(split[:, at], 'col', split_axis=0, concat_axis=0, tiled=True)  104 us
    all_to_all x2, waiting for transfers between devices, plane_body(): lax.all_to_all(second(part), 'col', split_axis=0, concat_axis=0, tiled=True)  99.7 us
    pallas_call x2, Pallas kernels, second(): pl.pallas_call(lambda *refs: transform_second(1.0 / length, *refs), out_s...  29.5 us
    pallas_call x2, Pallas kernels, first(): pl.pallas_call(transform_first, out_shape=jax.ShapeDtypeStruct((RADIX, 2,...  18.8 us
    pallas_call x2, Pallas kernels, first(): pl.pallas_call(symmetrize, out_shape=jax.ShapeDtypeStruct((1, RADIX, widt...  17.1 us
    pallas_call x2, Pallas kernels, widen(): pl.pallas_call(widen_kernel, out_shape=(shape, shape), grid=(owners,), in...  14.4 us
    all_to_all x2, starting transfers between devices, gather(): lax.all_to_all(split[:, at], 'col', split_axis=0, concat_axis=0, tiled=True)  11.3 us
  transfers between devices with their start and end apart: 4, of which 4 were waited for; matrix products, arithmetic and copies ran while one was open for 6% of the time, Pallas kernels for 25%

profile of v2, /device:TPU:0, one launch (start us, length us, event | category | flops | bytes accessed | tf_op | source)
XLA Modules:
  0.0 541.7 jit_solution(9283060567152939523)
XLA Ops:
  0.6 7.5 %slice_bitcast_fusion = (f32[8,512,256]{2,1,0:T(8,128)}, f32[8,512,256]{2,1,0:T(8,128)}) fusion(f32[8,2,512,256]{3,2,1,0:T(8,128)} %bitcast.33), kind=kLoop, calls=%fused_computation.14 | loop fusion | bytes 16777216 | tf_op jit(solution)/shard_map/squeeze | solution.py:417
  8.1 0.0 copy-start.1
  8.1 6.5 %all-to-all-start = ((f32[8,512,256]{2,1,0:T(8,128)}), f32[8,512,256]{2,1,0:T(8,128)}, u32[]{:S(2)}, u32[]{:S(2)}) async-start(f32[8,512,256]{2,1,0:T(8,128)} %get-tuple-element.15), calls=%async_computation | async-start | bytes 8388608 | tf_op jit(solution)/shard_map/all_to_all | solution.py:417
  14.6 0.1 compare_convert_fusion
  14.7 0.0 copy-done.1
  14.7 0.7 multiply_reduce_fusion
  15.4 0.6 convolution_convert_fusion.1
  16.0 1.2 copy.25
  17.3 0.5 convolution_convert_fusion
  17.8 2.4 copy.27
  20.3 0.3 fusion.40
  20.6 0.7 fusion.11.pick_ref
  21.3 0.6 fusion.34
  21.9 0.5 fusion.37
  22.4 1.1 fusion.26
  23.5 1.1 fusion.8
  24.6 4.6 multiply_subtract_fusion.1
  29.2 0.0 copy-start
  29.2 1.5 fusion.57
  30.7 0.9 copy-done
  31.6 1.4 fusion.56
  33.0 75.7 %all-to-all-done = f32[8,512,256]{2,1,0:T(8,128)} async-done(((f32[8,512,256]{2,1,0:T(8,128)}), f32[8,512,256]{2,1,0:T(8,128)}, u32[]{:S(2)}, u32[]{:S(2)}) %all-to-all-start) | async-done | bytes 4194336 | tf_op jit(solution)/shard_map/all_to_all | solution.py:417
  108.7 4.8 all-to-all-start.2
  113.5 5.1 reduce-precision_convert_fusion.2
  118.6 0.1 mul.674
  118.7 0.1 mul.685
  118.8 0.5 mul.688
  119.3 0.5 mul.682
  119.9 2.1 reduce-precision_convert_fusion.1
  122.0 3.9 pad_maximum_fusion.1.refs_1_
  125.9 3.8 pad_maximum_fusion.table_ref
  129.7 49.1 %shard_map.41 = f32[4,2,512,256]{3,2,1,0:T(8,128)} custom-call(f32[4,2,512,256]{3,2,1,0:T(8,128)} %bitcast.5.send_ref), custom_call_target="tpu_custom_call" | custom-call | flops 40000000000 | bytes 4194304 | tf_op jit(solution)/shard_map/pallas_call | solution.py:329
  178.9 28.4 %all-to-all-done.2 = f32[8,512,256]{2,1,0:T(8,128)} async-done(((f32[8,512,256]{2,1,0:T(8,128)}), f32[8,512,256]{2,1,0:T(8,128)}, u32[]{:S(2)}, u32[]{:S(2)}) %all-to-all-start.2) | async-done | bytes 4194336 | tf_op jit(solution)/shard_map/all_to_all | solution.py:417
  207.3 48.5 %shard_map.46 = f32[4,2,512,256]{3,2,1,0:T(8,128)} custom-call(f32[4,2,512,256]{3,2,1,0:T(8,128)} %bitcast.16.send_ref), custom_call_target="tpu_custom_call" | custom-call | flops 40000000000 | bytes 4194304 | tf_op jit(solution)/shard_map/pallas_call | solution.py:329
  255.8 8.5 %shard_map.47.sym_ref = bf16[1,4,512,512]{3,2,1,0:T(8,128)(2,1)} custom-call(f32[8,1,512,256]{3,2,1,0:T(8,128)} %bitcast.15.direct_ref, f32[4,2,1,512,256]{4,3,2,1,0:T(8,128)} %bitcast.41, bf16[1,2048,129]{2,1,0:T(8,128)(2,1)} %get-tuple-element.22.near_ref, bf16[1,2048,129]{2,1,0:T(8,128)(2,1)} %get-tuple-element.20.far_ref, ...), custom_call_target="tpu_custom_call" | custom-call | flops 14000000000 | bytes 10000000 | tf_op jit(solution)/shard_map/pallas_call | solution.py:420
  264.3 9.4 %shard_map.48.send_ref = bf16[4,2,1,512,512]{4,3,2,1,0:T(8,128)(2,1)} custom-call(bf16[4,4,512,512]{3,2,1,0:T(8,128)(2,1)} %pad_maximum_fusion.table_ref, bf16[1,4,512,512]{3,2,1,0:T(8,128)(2,1)} %shard_map.47.sym_ref), custom_call_target="tpu_custom_call" | custom-call | flops 14000000000 | bytes 10000000 | tf_op jit(solution)/shard_map/pallas_call | solution.py:447
  273.7 48.8 %shard_map.49.refs_0_ = bf16[4,2,1,512,512]{4,3,2,1,0:T(8,128)(2,1)} custom-call(bf16[4,2,1,512,512]{4,3,2,1,0:T(8,128)(2,1)} %shard_map.48.send_ref), custom_call_target="tpu_custom_call" | custom-call | flops 40000000000 | bytes 8388608 | tf_op jit(solution)/shard_map/pallas_call | solution.py:329
  322.6 14.8 %shard_map.50 = bf16[8,2,1,64,2048]{4,3,2,1,0:T(8,128)(2,1)} custom-call(bf16[4,2,1,512,512]{4,3,2,1,0:T(8,128)(2,1)} %shard_map.49.refs_0_, bf16[4,4,512,512]{3,2,1,0:T(8,128)(2,1)} %pad_maximum_fusion.1.refs_1_), custom_call_target="tpu_custom_call" | custom-call | flops 14000000000 | bytes 10000000 | tf_op jit(solution)/shard_map/pallas_call | solution.py:463
  337.4 4.8 all-to-all-start.3
  342.2 8.6 %shard_map.42.sym_ref = bf16[1,4,512,512]{3,2,1,0:T(8,128)(2,1)} custom-call(f32[8,1,512,256]{3,2,1,0:T(8,128)} %bitcast.4.direct_ref, f32[4,2,1,512,256]{4,3,2,1,0:T(8,128)} %bitcast.40, bf16[1,2048,129]{2,1,0:T(8,128)(2,1)} %get-tuple-element.23.near_ref, bf16[1,2048,129]{2,1,0:T(8,128)(2,1)} %get-tuple-element.21.far_ref, ...), custom_call_target="tpu_custom_call" | custom-call | flops 14000000000 | bytes 10000000 | tf_op jit(solution)/shard_map/pallas_call | solution.py:420
  350.7 9.4 %shard_map.43.send_ref = bf16[4,2,1,512,512]{4,3,2,1,0:T(8,128)(2,1)} custom-call(bf16[4,4,512,512]{3,2,1,0:T(8,128)(2,1)} %pad_maximum_fusion.table_ref, bf16[1,4,512,512]{3,2,1,0:T(8,128)(2,1)} %shard_map.42.sym_ref), custom_call_target="tpu_custom_call" | custom-call | flops 14000000000 | bytes 10000000 | tf_op jit(solution)/shard_map/pallas_call | solution.py:447
  360.1 48.1 %shard_map.44.refs_0_ = bf16[4,2,1,512,512]{4,3,2,1,0:T(8,128)(2,1)} custom-call(bf16[4,2,1,512,512]{4,3,2,1,0:T(8,128)(2,1)} %shard_map.43.send_ref), custom_call_target="tpu_custom_call" | custom-call | flops 40000000000 | bytes 8388608 | tf_op jit(solution)/shard_map/pallas_call | solution.py:329
  408.2 14.8 %shard_map.45 = bf16[8,2,1,64,2048]{4,3,2,1,0:T(8,128)(2,1)} custom-call(bf16[4,2,1,512,512]{4,3,2,1,0:T(8,128)(2,1)} %shard_map.44.refs_0_, bf16[4,4,512,512]{3,2,1,0:T(8,128)(2,1)} %pad_maximum_fusion.1.refs_1_), custom_call_target="tpu_custom_call" | custom-call | flops 14000000000 | bytes 10000000 | tf_op jit(solution)/shard_map/pallas_call | solution.py:463
  423.0 12.9 %all-to-all-done.3.got_ref = bf16[8,2,1,64,2048]{4,3,2,1,0:T(8,128)(2,1)} async-done(((bf16[8,2,1,64,2048]{4,3,2,1,0:T(8,128)(2,1)}), bf16[8,2,1,64,2048]{4,3,2,1,0:T(8,128)(2,1)}, u32[]{:S(2)}, u32[]{:S(2)}) %all-to-all-start.3) | async-done | bytes 4194336 | tf_op jit(solution)/shard_map/all_to_all | solution.py:486
  435.9 4.6 all-to-all-start.1
  440.5 7.2 %shard_map.51 = (f32[8,2,64,2048]{3,2,1,0:T(8,128)}, f32[8,2,64,2048]{3,2,1,0:T(8,128)}) custom-call(bf16[8,2,1,64,2048]{4,3,2,1,0:T(8,128)(2,1)} %all-to-all-done.3.got_ref), custom_call_target="tpu_custom_call" | custom-call | flops 8000000000 | bytes 12582912 | tf_op jit(solution)/shard_map/pallas_call | solution.py:357
  447.7 86.8 %all-to-all-done.1.got_ref = bf16[8,2,1,64,2048]{4,3,2,1,0:T(8,128)(2,1)} async-done(((bf16[8,2,1,64,2048]{4,3,2,1,0:T(8,128)(2,1)}), bf16[8,2,1,64,2048]{4,3,2,1,0:T(8,128)(2,1)}, u32[]{:S(2)}, u32[]{:S(2)}) %all-to-all-start.1) | async-done | bytes 4194336 | tf_op jit(solution)/shard_map/all_to_all | solution.py:486
  534.5 7.2 %shard_map.52 = (f32[8,2,64,2048]{3,2,1,0:T(8,128)}, f32[8,2,64,2048]{3,2,1,0:T(8,128)}) custom-call(bf16[8,2,1,64,2048]{4,3,2,1,0:T(8,128)(2,1)} %all-to-all-done.1.got_ref, f32[8,2,64,2048]{3,2,1,0:T(8,128)} %get-tuple-element.6.refs_0_, f32[8,2,64,2048]{3,2,1,0:T(8,128)} %get-tuple-element.7.refs_1_), custom_call_target="tpu_custom_call", output_to_operand_aliasing={{0}: (1, {}), {1}: (2, {})} | custom-call | flops 8000000000 | bytes 12582912 | tf_op jit(solution)/shard_map/pallas_call | solution.py:357
  (10 shorter events, 0.1 us)
Async XLA Ops:
  8.1 6.6 %copy-start.1 = (s32[2,129,129]{2,0,1:T(2,128)S(1)}, s32[2,129,129]{2,0,1:T(2,128)}, u32[]{:S(2)}) copy-start(s32[2,129,129]{2,0,1:T(2,128)} %param.3) | copy-start | bytes 399388
  8.1 100.6 %all-to-all-start = ((f32[8,512,256]{2,1,0:T(8,128)}), f32[8,512,256]{2,1,0:T(8,128)}, u32[]{:S(2)}, u32[]{:S(2)}) async-start(f32[8,512,256]{2,1,0:T(8,128)} %get-tuple-element.15), calls=%async_computation | async-start | bytes 8388608 | tf_op jit(solution)/shard_map/all_to_all | solution.py:417
  29.2 2.3 copy-start
  108.7 98.6 %all-to-all-start.2 = ((f32[8,512,256]{2,1,0:T(8,128)}), f32[8,512,256]{2,1,0:T(8,128)}, u32[]{:S(2)}, u32[]{:S(2)}) async-start(f32[8,512,256]{2,1,0:T(8,128)} %get-tuple-element.14), calls=%async_computation.2 | async-start | bytes 8388608 | tf_op jit(solution)/shard_map/all_to_all | solution.py:417
  337.4 98.6 %all-to-all-start.3 = ((bf16[8,2,1,64,2048]{4,3,2,1,0:T(8,128)(2,1)}), bf16[8,2,1,64,2048]{4,3,2,1,0:T(8,128)(2,1)}, u32[]{:S(2)}, u32[]{:S(2)}) async-start(bf16[8,2,1,64,2048]{4,3,2,1,0:T(8,128)(2,1)} %shard_map.50), calls=%async_computation.3 | async-start | bytes 8388608 | tf_op jit(solution)/shard_map/all_to_all | solution.py:486
  435.9 98.5 %all-to-all-start.1 = ((bf16[8,2,1,64,2048]{4,3,2,1,0:T(8,128)(2,1)}), bf16[8,2,1,64,2048]{4,3,2,1,0:T(8,128)(2,1)}, u32[]{:S(2)}, u32[]{:S(2)}) async-start(bf16[8,2,1,64,2048]{4,3,2,1,0:T(8,128)(2,1)} %shard_map.45), calls=%async_computation.1 | async-start | bytes 8388608 | tf_op jit(solution)/shard_map/all_to_all | solution.py:486

commit v3 on v2

--- a/solution.py
+++ b/solution.py
@@ -162,6 +162,7 @@
 
 
 RADIX = 4
+SHARES = 2
 
 
 def spin(first_ids, second_ids, period):
@@ -183,7 +184,7 @@
     return jnp.stack([*halves(full_re), *halves(full_im)])
 
 
-def twiddles(length):
+def twiddles(length, owners, shares):
     width = length // RADIX
     fine = 16
     ids = jnp.arange(width, dtype=jnp.int32)
@@ -193,7 +194,9 @@
     minor = ids[None, None, None, :]
     shape = (RADIX, width, width)
     sample = RADIX * minor + lead
-    freq_major = packed(spin(sample, high_ids, length), spin(sample, low_ids, length), shape)
+    block = high_ids.reshape(owners, shares, -1)
+    turned = jnp.swapaxes(block, 0, 1).reshape(high_ids.shape)
+    freq_major = packed(spin(sample, turned, length), spin(sample, low_ids, length), shape)
     time_major = packed(
         spin(RADIX * high_ids, minor, length), spin(RADIX * low_ids + lead, minor, length), shape
     )
@@ -350,10 +353,10 @@
     im_ref[0, 0] = got_ref[0, 1, 0].astype(jnp.float32)
 
 
-def widen(at, held, received, outs):
+def widen(at, share, held, received, outs):
     owners, _, _, rows, length = received.shape
-    shape = jax.ShapeDtypeStruct((owners, held, rows, length), jnp.float32)
-    spec = pl.BlockSpec((1, 1, rows, length), lambda c: (c, at, 0, 0))
+    shape = jax.ShapeDtypeStruct((owners, held, rows * SHARES, length), jnp.float32)
+    spec = pl.BlockSpec((1, 1, rows, length), lambda c: (c, at, share, 0))
     return pl.pallas_call(
         widen_kernel,
         out_shape=(shape, shape),
@@ -405,19 +408,20 @@
     source = RADIX * (local % piece) + local // piece
     order = (source[:, None] == local[None, :]).astype(bf16)
     flip = (source[None, :] == local[:, None]).astype(bf16)
-    freq_major, time_major = twiddles(length)
-
-    tile = min(128, width)
-    owners = max(1, tile // freq_width)
-    rows = owners * freq_width
+    freq_major, time_major = twiddles(length, col_count, SHARES)
+
+    span = freq_width // SHARES
+    part_rows = width // SHARES
+    tile = min(128, part_rows)
+    owners = tile // span
     params = pltpu.CompilerParams(vmem_limit_bytes=LIMIT)
     split = intensity.reshape(col_count, held, h_block, k_block)
 
     def gather(at):
         return lax.all_to_all(split[:, at], "col", split_axis=0, concat_axis=0, tiled=True)
 
-    def first(at, direct, mirror):
-        sym = pl.pallas_call(
+    def blend(at, direct, mirror):
+        return pl.pallas_call(
             symmetrize,
             out_shape=jax.ShapeDtypeStruct((1, RADIX, width, h_block), bf16),
             grid=(1, row_count),
@@ -444,12 +448,15 @@
             order,
             flip,
         )
+
+    def first(share, sym):
+        skip = share * (part_rows // tile)
         return pl.pallas_call(
             transform_first,
-            out_shape=jax.ShapeDtypeStruct((RADIX, 2, 1, width, h_block), bf16),
-            grid=(width // tile, 1),
+            out_shape=jax.ShapeDtypeStruct((RADIX, 2, 1, part_rows, h_block), bf16),
+            grid=(part_rows // tile, 1),
             in_specs=[
-                pl.BlockSpec((4, RADIX, tile, width), lambda d, p: (0, 0, d, 0)),
+                pl.BlockSpec((4, RADIX, tile, width), lambda d, p: (0, 0, d + skip, 0)),
                 pl.BlockSpec((1, RADIX, width, h_block), lambda d, p: (p, 0, 0, 0)),
             ],
             out_specs=pl.BlockSpec((RADIX, 2, 1, tile, h_block), lambda d, p: (0, 0, p, d, 0)),
@@ -462,14 +469,14 @@
     def second(parts):
         return pl.pallas_call(
             lambda *refs: transform_second(1.0 / length, *refs),
-            out_shape=jax.ShapeDtypeStruct((col_count, 2, 1, freq_width, length), bf16),
-            grid=(1, width // rows),
+            out_shape=jax.ShapeDtypeStruct((col_count, 2, 1, span, length), bf16),
+            grid=(1, part_rows // tile),
             in_specs=[
-                pl.BlockSpec((row_count, 2, 1, rows, h_block), lambda p, d: (0, 0, p, d, 0)),
+                pl.BlockSpec((row_count, 2, 1, tile, h_block), lambda p, d: (0, 0, p, d, 0)),
                 pl.BlockSpec((4, RADIX, width, width), lambda p, d: (0, 0, 0, 0)),
             ],
             out_specs=pl.BlockSpec(
-                (owners, 2, 1, freq_width, length), lambda p, d: (d, 0, p, 0, 0)
+                (owners, 2, 1, span, length), lambda p, d: (d, 0, p, 0, 0)
             ),
             compiler_params=params,
             cost_estimate=pl.CostEstimate(
@@ -477,18 +484,32 @@
             ),
         )(parts, time_major)
 
+    def deliver(sent):
+        return lax.all_to_all(sent, "col", split_axis=0, concat_axis=0, tiled=True)
+
     directs = [gather(at) for at in range(held)]
-    mirrors = [
-        swap(direct.reshape(row_count, groups, h_block, k_block), 0) for direct in directs
-    ]
-    parts = [swap(first(at, directs[at], mirrors[at]), 1) for at in range(held)]
-    spectra = [
-        lax.all_to_all(second(part), "col", split_axis=0, concat_axis=0, tiled=True)
-        for part in parts
-    ]
-    outs = ()
-    for at, received in enumerate(spectra):
-        outs = widen(at, held, received, outs)
+    outs, waiting = (), None
+    for at in range(held):
+        direct = directs[at]
+        mirror = swap(direct.reshape(row_count, groups, h_block, k_block), 0)
+        if waiting is not None:
+            mirror, received = lax.optimization_barrier((mirror, waiting[2]))
+            outs = widen(waiting[0], waiting[1], held, received, outs)
+        sym = blend(at, direct, mirror)
+        waiting = None
+        for share in range(SHARES):
+            sent = second(swap(first(share, sym), 1))
+            if at + 1 < held:
+                sym, sent, directs[at + 1] = lax.optimization_barrier(
+                    (sym, sent, directs[at + 1])
+                )
+            else:
+                sym, sent = lax.optimization_barrier((sym, sent))
+            received = deliver(sent)
+            if share == 0 and at + 1 < held:
+                waiting = (at, share, received)
+            else:
+                outs = widen(at, share, held, received, outs)
     return tuple(half.reshape(planes, freq_width, length) for half in outs)
 
 

time: 543 us -> 484 us (0.89)
  waiting for transfers between devices: 204 us -> 110 us
  Pallas kernels: 274 us -> 307 us
  starting transfers between devices: 20.6 us -> 29.8 us
  other arithmetic: 24.7 us -> 18.1 us
    all_to_all x2 -> x4, waiting for transfers between devices: 99.7 us -> 43.6 us  [deliver(): return lax.all_to_all(sent, 'col', split_axis=0, concat_axis=0, tiled=True)]
    all_to_all x2, waiting for transfers between devices: 104 us -> 66.5 us  [gather(): lax.all_to_all(split[:, at], 'col', split_axis=0, concat_axis=0, tiled=True)]
    pallas_call x2 -> x4, Pallas kernels: 14.4 us -> 23.8 us  [widen(): pl.pallas_call(widen_kernel, out_shape=(shape, shape), grid=(owners,), in...]
    pallas_call x2 -> x4, Pallas kernels: 29.5 us -> 38.9 us  [second(): pl.pallas_call(lambda *refs: transform_second(1.0 / length, *refs), out_s...]
    all_to_all x2 -> x4, starting transfers between devices: 9.38 us -> 18.6 us  [deliver(): return lax.all_to_all(sent, 'col', split_axis=0, concat_axis=0, tiled=True)]
    pallas_call x4 -> x6, Pallas kernels: 195 us -> 203 us  [swap(): pl.pallas_call(swap_kernel, out_shape=jax.ShapeDtypeStruct(values.shape,...]
    pallas_call x2 -> x4, Pallas kernels: 18.8 us -> 23.7 us  [first(): pl.pallas_call(transform_first, out_shape=jax.ShapeDtypeStruct((RADIX, 2,...]
  transfers between devices with their start and end apart: 4 -> 6, of which waited for: 4 -> 3; matrix products, arithmetic and copies ran while one was open for 6% -> 6% of each run, Pallas kernels for 25% -> 62%
where the time goes in v3:
time: 484 us; the launch traced here: 483 us
  Pallas kernels  307 us (63%)
  waiting for transfers between devices  110 us (23%)
  starting transfers between devices  29.8 us (6%)
  other arithmetic  18.1 us (4%)
  local copies, waits for them, and re-layouts  15.6 us (3%)
    pallas_call x6, Pallas kernels, swap(): pl.pallas_call(swap_kernel, out_shape=jax.ShapeDtypeStruct(values.shape,...  203 us
    all_to_all x2, waiting for transfers between devices, gather(): lax.all_to_all(split[:, at], 'col', split_axis=0, concat_axis=0, tiled=True)  66.5 us
    all_to_all x4, waiting for transfers between devices, deliver(): return lax.all_to_all(sent, 'col', split_axis=0, concat_axis=0, tiled=True)  43.6 us
    pallas_call x4, Pallas kernels, second(): pl.pallas_call(lambda *refs: transform_second(1.0 / length, *refs), out_s...  38.9 us
    pallas_call x4, Pallas kernels, widen(): pl.pallas_call(widen_kernel, out_shape=(shape, shape), grid=(owners,), in...  23.8 us
    pallas_call x4, Pallas kernels, first(): pl.pallas_call(transform_first, out_shape=jax.ShapeDtypeStruct((RADIX, 2,...  23.7 us
    all_to_all x4, starting transfers between devices, deliver(): return lax.all_to_all(sent, 'col', split_axis=0, concat_axis=0, tiled=True)  18.6 us
    pallas_call x2, Pallas kernels, blend(): pl.pallas_call(symmetrize, out_shape=jax.ShapeDtypeStruct((1, RADIX, widt...  17.1 us
  transfers between devices with their start and end apart: 6, of which 3 were waited for; matrix products, arithmetic and copies ran while one was open for 6% of the time, Pallas kernels for 62%

profile of v3, /device:TPU:0, one launch (start us, length us, event | category | flops | bytes accessed | tf_op | source)
XLA Modules:
  0.0 482.6 jit_solution(11045358589186474716)
XLA Ops:
  0.6 7.5 %slice_bitcast_fusion = (f32[8,512,256]{2,1,0:T(8,128)}, f32[8,512,256]{2,1,0:T(8,128)}) fusion(f32[8,2,512,256]{3,2,1,0:T(8,128)} %bitcast.33), kind=kLoop, calls=%fused_computation.14 | loop fusion | bytes 16777216 | tf_op jit(solution)/shard_map/squeeze | solution.py:421
  8.1 0.0 copy-start.3
  8.1 6.5 %all-to-all-start = ((f32[8,512,256]{2,1,0:T(8,128)}), f32[8,512,256]{2,1,0:T(8,128)}, u32[]{:S(2)}, u32[]{:S(2)}) async-start(f32[8,512,256]{2,1,0:T(8,128)} %get-tuple-element.43), calls=%async_computation | async-start | bytes 8388608 | tf_op jit(solution)/shard_map/all_to_all | solution.py:421
  14.7 0.1 compare_convert_fusion
  14.7 0.0 copy-done.3
  14.7 0.7 multiply_reduce_fusion
  15.5 0.5 convolution_convert_fusion
  16.0 0.6 convolution_convert_fusion.1
  16.6 0.1 mul.656
  16.7 2.4 copy.29
  19.1 1.2 copy.31
  20.3 0.3 fusion.40
  20.7 0.7 fusion.11.pick_ref
  21.3 0.6 fusion.34
  21.9 0.5 fusion.37
  22.5 1.1 fusion.26
  23.6 1.1 fusion.8
  24.7 0.0 copy-start
  24.7 1.3 multiply_subtract_fusion.1
  26.1 0.2 copy-done
  26.3 1.5 fusion.57
  27.8 1.4 fusion.56
  29.3 1.7 reduce-precision_convert_fusion.2
  31.0 0.1 mul.680
  31.1 0.1 mul.691
  31.2 0.5 mul.694
  31.7 0.5 mul.688
  32.3 2.1 reduce-precision_convert_fusion.1
  34.4 3.9 pad_maximum_fusion.1.refs_1_
  38.3 3.8 pad_maximum_fusion.table_ref
  42.2 66.5 %all-to-all-done = f32[8,512,256]{2,1,0:T(8,128)} async-done(((f32[8,512,256]{2,1,0:T(8,128)}), f32[8,512,256]{2,1,0:T(8,128)}, u32[]{:S(2)}, u32[]{:S(2)}) %all-to-all-start) | async-done | bytes 4194336 | tf_op jit(solution)/shard_map/all_to_all | solution.py:421
  108.7 4.7 all-to-all-start.1
  113.4 49.1 %shard_map.41 = f32[4,2,512,256]{3,2,1,0:T(8,128)} custom-call(f32[4,2,512,256]{3,2,1,0:T(8,128)} %bitcast.3.send_ref), custom_call_target="tpu_custom_call" | custom-call | flops 40000000000 | bytes 4194304 | tf_op jit(solution)/shard_map/pallas_call | solution.py:332
  162.6 8.6 %shard_map.42.sym_ref = bf16[1,4,512,512]{3,2,1,0:T(8,128)(2,1)} custom-call(f32[8,1,512,256]{3,2,1,0:T(8,128)} %bitcast.2.direct_ref, f32[4,2,1,512,256]{4,3,2,1,0:T(8,128)} %bitcast.41, bf16[1,2048,129]{2,1,0:T(8,128)(2,1)} %get-tuple-element.51.near_ref, bf16[1,2048,129]{2,1,0:T(8,128)(2,1)} %get-tuple-element.49.far_ref, ...), custom_call_target="tpu_custom_call" | custom-call | flops 14000000000 | bytes 10000000 | tf_op jit(solution)/shard_map/pallas_call | solution.py:424
  171.2 5.9 %shard_map.43.send_ref = bf16[4,2,1,256,512]{4,3,2,1,0:T(8,128)(2,1)} custom-call(bf16[4,4,512,512]{3,2,1,0:T(8,128)(2,1)} %pad_maximum_fusion.table_ref, bf16[1,4,512,512]{3,2,1,0:T(8,128)(2,1)} %shard_map.42.sym_ref), custom_call_target="tpu_custom_call" | custom-call | flops 14000000000 | bytes 10000000 | tf_op jit(solution)/shard_map/pallas_call | solution.py:454
  177.1 26.4 %shard_map.44.refs_0_ = bf16[4,2,1,256,512]{4,3,2,1,0:T(8,128)(2,1)} custom-call(bf16[4,2,1,256,512]{4,3,2,1,0:T(8,128)(2,1)} %shard_map.43.send_ref), custom_call_target="tpu_custom_call" | custom-call | flops 40000000000 | bytes 4194304 | tf_op jit(solution)/shard_map/pallas_call | solution.py:332
  203.5 9.7 %shard_map.45 = bf16[8,2,1,32,2048]{4,3,2,1,0:T(8,128)(2,1)} custom-call(bf16[4,2,1,256,512]{4,3,2,1,0:T(8,128)(2,1)} %shard_map.44.refs_0_, bf16[4,4,512,512]{3,2,1,0:T(8,128)(2,1)} %pad_maximum_fusion.1.refs_1_), custom_call_target="tpu_custom_call" | custom-call | flops 14000000000 | bytes 10000000 | tf_op jit(solution)/shard_map/pallas_call | solution.py:470
  213.3 0.0 all-to-all-done.1
  213.3 4.8 all-to-all-start.2
  218.0 5.9 %shard_map.46.send_ref = bf16[4,2,1,256,512]{4,3,2,1,0:T(8,128)(2,1)} custom-call(bf16[4,4,512,512]{3,2,1,0:T(8,128)(2,1)} %pad_maximum_fusion.table_ref, bf16[1,4,512,512]{3,2,1,0:T(8,128)(2,1)} %shard_map.42.sym_ref), custom_call_target="tpu_custom_call" | custom-call | flops 14000000000 | bytes 10000000 | tf_op jit(solution)/shard_map/pallas_call | solution.py:454
  224.0 26.0 %shard_map.47.refs_0_ = bf16[4,2,1,256,512]{4,3,2,1,0:T(8,128)(2,1)} custom-call(bf16[4,2,1,256,512]{4,3,2,1,0:T(8,128)(2,1)} %shard_map.46.send_ref), custom_call_target="tpu_custom_call" | custom-call | flops 40000000000 | bytes 4194304 | tf_op jit(solution)/shard_map/pallas_call | solution.py:332
  250.0 9.7 %shard_map.48 = bf16[8,2,1,32,2048]{4,3,2,1,0:T(8,128)(2,1)} custom-call(bf16[4,2,1,256,512]{4,3,2,1,0:T(8,128)(2,1)} %shard_map.47.refs_0_, bf16[4,4,512,512]{3,2,1,0:T(8,128)(2,1)} %pad_maximum_fusion.1.refs_1_), custom_call_target="tpu_custom_call" | custom-call | flops 14000000000 | bytes 10000000 | tf_op jit(solution)/shard_map/pallas_call | solution.py:470
  259.7 48.8 %shard_map.49 = f32[4,2,512,256]{3,2,1,0:T(8,128)} custom-call(f32[4,2,512,256]{3,2,1,0:T(8,128)} %bitcast.16.send_ref), custom_call_target="tpu_custom_call" | custom-call | flops 40000000000 | bytes 4194304 | tf_op jit(solution)/shard_map/pallas_call | solution.py:332
  308.6 0.0 all-to-all-done.2.got_ref
  308.6 0.0 copy-start.1
  308.6 4.7 all-to-all-start.5
  313.3 8.5 %shard_map.50.sym_ref = bf16[1,4,512,512]{3,2,1,0:T(8,128)(2,1)} custom-call(f32[8,1,512,256]{3,2,1,0:T(8,128)} %bitcast.15.direct_ref, f32[4,2,1,512,256]{4,3,2,1,0:T(8,128)} %bitcast.40, bf16[1,2048,129]{2,1,0:T(8,128)(2,1)} %get-tuple-element.50.near_ref, bf16[1,2048,129]{2,1,0:T(8,128)(2,1)} %get-tuple-element.48.far_ref, ...), custom_call_target="tpu_custom_call" | custom-call | flops 14000000000 | bytes 10000000 | tf_op jit(solution)/shard_map/pallas_call | solution.py:424
  321.9 0.0 copy-done.1
  321.9 5.9 %shard_map.51.send_ref = bf16[4,2,1,256,512]{4,3,2,1,0:T(8,128)(2,1)} custom-call(bf16[4,4,512,512]{3,2,1,0:T(8,128)(2,1)} %pad_maximum_fusion.table_ref, bf16[1,4,512,512]{3,2,1,0:T(8,128)(2,1)} %shard_map.50.sym_ref), custom_call_target="tpu_custom_call" | custom-call | flops 14000000000 | bytes 10000000 | tf_op jit(solution)/shard_map/pallas_call | solution.py:454
  327.8 26.1 %shard_map.52.refs_0_ = bf16[4,2,1,256,512]{4,3,2,1,0:T(8,128)(2,1)} custom-call(bf16[4,2,1,256,512]{4,3,2,1,0:T(8,128)(2,1)} %shard_map.51.send_ref), custom_call_target="tpu_custom_call" | custom-call | flops 40000000000 | bytes 4194304 | tf_op jit(solution)/shard_map/pallas_call | solution.py:332
  353.9 9.7 %shard_map.53 = bf16[8,2,1,32,2048]{4,3,2,1,0:T(8,128)(2,1)} custom-call(bf16[4,2,1,256,512]{4,3,2,1,0:T(8,128)(2,1)} %shard_map.52.refs_0_, bf16[4,4,512,512]{3,2,1,0:T(8,128)(2,1)} %pad_maximum_fusion.1.refs_1_), custom_call_target="tpu_custom_call" | custom-call | flops 14000000000 | bytes 10000000 | tf_op jit(solution)/shard_map/pallas_call | solution.py:470
  363.7 5.9 %shard_map.54.send_ref = bf16[4,2,1,256,512]{4,3,2,1,0:T(8,128)(2,1)} custom-call(bf16[4,4,512,512]{3,2,1,0:T(8,128)(2,1)} %pad_maximum_fusion.table_ref, bf16[1,4,512,512]{3,2,1,0:T(8,128)(2,1)} %shard_map.50.sym_ref), custom_call_target="tpu_custom_call" | custom-call | flops 14000000000 | bytes 10000000 | tf_op jit(solution)/shard_map/pallas_call | solution.py:454
  369.6 0.0 all-to-all-done.5.got_ref
  369.6 4.7 all-to-all-start.4
  374.3 26.9 %shard_map.55.refs_0_ = bf16[4,2,1,256,512]{4,3,2,1,0:T(8,128)(2,1)} custom-call(bf16[4,2,1,256,512]{4,3,2,1,0:T(8,128)(2,1)} %shard_map.54.send_ref), custom_call_target="tpu_custom_call" | custom-call | flops 40000000000 | bytes 4194304 | tf_op jit(solution)/shard_map/pallas_call | solution.py:332
  401.1 9.7 %shard_map.56 = bf16[8,2,1,32,2048]{4,3,2,1,0:T(8,128)(2,1)} custom-call(bf16[4,2,1,256,512]{4,3,2,1,0:T(8,128)(2,1)} %shard_map.55.refs_0_, bf16[4,4,512,512]{3,2,1,0:T(8,128)(2,1)} %pad_maximum_fusion.1.refs_1_), custom_call_target="tpu_custom_call" | custom-call | flops 14000000000 | bytes 10000000 | tf_op jit(solution)/shard_map/pallas_call | solution.py:470
  410.8 12.5 %all-to-all-done.4.got_ref = bf16[8,2,1,32,2048]{4,3,2,1,0:T(8,128)(2,1)S(1)} async-done(((bf16[8,2,1,32,2048]{4,3,2,1,0:T(8,128)(2,1)}), bf16[8,2,1,32,2048]{4,3,2,1,0:T(8,128)(2,1)S(1)}, u32[]{:S(2)}, u32[]{:S(2)}) %all-to-all-start.4) | async-done | bytes 2097184 | tf_op jit(solution)/shard_map/all_to_all | solution.py:488
  423.3 4.3 all-to-all-start.3
  427.7 6.0 %shard_map.57 = (f32[8,2,64,2048]{3,2,1,0:T(8,128)}, f32[8,2,64,2048]{3,2,1,0:T(8,128)}) custom-call(bf16[8,2,1,32,2048]{4,3,2,1,0:T(8,128)(2,1)} %all-to-all-done.5.got_ref), custom_call_target="tpu_custom_call" | custom-call | flops 8000000000 | bytes 6291456 | tf_op jit(solution)/shard_map/pallas_call | solution.py:360
  433.6 0.0 copy-done.2
  433.6 6.0 %shard_map.58 = (f32[8,2,64,2048]{3,2,1,0:T(8,128)}, f32[8,2,64,2048]{3,2,1,0:T(8,128)}) custom-call(bf16[8,2,1,32,2048]{4,3,2,1,0:T(8,128)(2,1)} %copy-done.1, f32[8,2,64,2048]{3,2,1,0:T(8,128)} %get-tuple-element.30.refs_0_, f32[8,2,64,2048]{3,2,1,0:T(8,128)} %get-tuple-element.31.refs_1_), custom_call_target="tpu_custom_call", output_to_operand_aliasing={{0}: (1, {}), {1}: (2, {})} | custom-call | flops 8000000000 | bytes 6291456 | tf_op jit(solution)/shard_map/pallas_call | solution.py:360
  439.6 6.0 %shard_map.59 = (f32[8,2,64,2048]{3,2,1,0:T(8,128)}, f32[8,2,64,2048]{3,2,1,0:T(8,128)}) custom-call(bf16[8,2,1,32,2048]{4,3,2,1,0:T(8,128)(2,1)} %copy-done.2, f32[8,2,64,2048]{3,2,1,0:T(8,128)} %get-tuple-element.32.refs_0_, f32[8,2,64,2048]{3,2,1,0:T(8,128)} %get-tuple-element.33.refs_1_), custom_call_target="tpu_custom_call", output_to_operand_aliasing={{0}: (1, {}), {1}: (2, {})} | custom-call | flops 8000000000 | bytes 6291456 | tf_op jit(solution)/shard_map/pallas_call | solution.py:360
  445.5 31.2 %all-to-all-done.3.got_ref = bf16[8,2,1,32,2048]{4,3,2,1,0:T(8,128)(2,1)} async-done(((bf16[8,2,1,32,2048]{4,3,2,1,0:T(8,128)(2,1)}), bf16[8,2,1,32,2048]{4,3,2,1,0:T(8,128)(2,1)}, u32[]{:S(2)}, u32[]{:S(2)}) %all-to-all-start.3) | async-done | bytes 2097184 | tf_op jit(solution)/shard_map/all_to_all | solution.py:488
  476.7 6.0 %shard_map.60 = (f32[8,2,64,2048]{3,2,1,0:T(8,128)}, f32[8,2,64,2048]{3,2,1,0:T(8,128)}) custom-call(bf16[8,2,1,32,2048]{4,3,2,1,0:T(8,128)(2,1)} %all-to-all-done.3.got_ref, f32[8,2,64,2048]{3,2,1,0:T(8,128)} %get-tuple-element.34.refs_0_, f32[8,2,64,2048]{3,2,1,0:T(8,128)} %get-tuple-element.35.refs_1_), custom_call_target="tpu_custom_call", output_to_operand_aliasing={{0}: (1, {}), {1}: (2, {})} | custom-call | flops 8000000000 | bytes 6291456 | tf_op jit(solution)/shard_map/pallas_call | solution.py:360
  (11 shorter events, 0.1 us)
Async XLA Ops:
  8.1 6.6 %copy-start.3 = (s32[2,129,129]{2,0,1:T(2,128)S(1)}, s32[2,129,129]{2,0,1:T(2,128)}, u32[]{:S(2)}) copy-start(s32[2,129,129]{2,0,1:T(2,128)} %param.3) | copy-start | bytes 399388
  8.1 100.6 %all-to-all-start = ((f32[8,512,256]{2,1,0:T(8,128)}), f32[8,512,256]{2,1,0:T(8,128)}, u32[]{:S(2)}, u32[]{:S(2)}) async-start(f32[8,512,256]{2,1,0:T(8,128)} %get-tuple-element.43), calls=%async_computation | async-start | bytes 8388608 | tf_op jit(solution)/shard_map/all_to_all | solution.py:421
  24.7 1.6 copy-start
  108.7 104.6 %all-to-all-start.1 = ((f32[8,512,256]{2,1,0:T(8,128)}), f32[8,512,256]{2,1,0:T(8,128)}, u32[]{:S(2)}, u32[]{:S(2)}) async-start(f32[8,512,256]{2,1,0:T(8,128)} %get-tuple-element.42), calls=%async_computation.1 | async-start | bytes 8388608 | tf_op jit(solution)/shard_map/all_to_all | solution.py:421
  213.3 95.3 %all-to-all-start.2 = ((bf16[8,2,1,32,2048]{4,3,2,1,0:T(8,128)(2,1)}), bf16[8,2,1,32,2048]{4,3,2,1,0:T(8,128)(2,1)S(1)}, u32[]{:S(2)}, u32[]{:S(2)}) async-start(bf16[8,2,1,32,2048]{4,3,2,1,0:T(8,128)(2,1)} %shard_map.45), calls=%async_computation.2 | async-start | bytes 4194304 | tf_op jit(solution)/shard_map/all_to_all | solution.py:488
  308.6 13.3 %copy-start.1 = (bf16[8,2,1,32,2048]{4,3,2,1,0:T(8,128)(2,1)}, bf16[8,2,1,32,2048]{4,3,2,1,0:T(8,128)(2,1)S(1)}, u32[]{:S(2)}) copy-start(bf16[8,2,1,32,2048]{4,3,2,1,0:T(8,128)(2,1)S(1)} %all-to-all-done.2.got_ref) | copy-start | bytes 6291460
  308.6 61.0 %all-to-all-start.5 = ((bf16[8,2,1,32,2048]{4,3,2,1,0:T(8,128)(2,1)}), bf16[8,2,1,32,2048]{4,3,2,1,0:T(8,128)(2,1)}, u32[]{:S(2)}, u32[]{:S(2)}) async-start(bf16[8,2,1,32,2048]{4,3,2,1,0:T(8,128)(2,1)} %shard_map.48), calls=%async_computation.5 | async-start | bytes 4194304 | tf_op jit(solution)/shard_map/all_to_all | solution.py:488
  369.6 53.7 %all-to-all-start.4 = ((bf16[8,2,1,32,2048]{4,3,2,1,0:T(8,128)(2,1)}), bf16[8,2,1,32,2048]{4,3,2,1,0:T(8,128)(2,1)S(1)}, u32[]{:S(2)}, u32[]{:S(2)}) async-start(bf16[8,2,1,32,2048]{4,3,2,1,0:T(8,128)(2,1)} %shard_map.53), calls=%async_computation.4 | async-start | bytes 4194304 | tf_op jit(solution)/shard_map/all_to_all | solution.py:488
  423.3 10.3 %copy-start.2 = (bf16[8,2,1,32,2048]{4,3,2,1,0:T(8,128)(2,1)}, bf16[8,2,1,32,2048]{4,3,2,1,0:T(8,128)(2,1)S(1)}, u32[]{:S(2)}) copy-start(bf16[8,2,1,32,2048]{4,3,2,1,0:T(8,128)(2,1)S(1)} %all-to-all-done.4.got_ref) | copy-start | bytes 6291460
  423.3 53.4 %all-to-all-start.3 = ((bf16[8,2,1,32,2048]{4,3,2,1,0:T(8,128)(2,1)}), bf16[8,2,1,32,2048]{4,3,2,1,0:T(8,128)(2,1)}, u32[]{:S(2)}, u32[]{:S(2)}) async-start(bf16[8,2,1,32,2048]{4,3,2,1,0:T(8,128)(2,1)} %shard_map.56), calls=%async_computation.3 | async-start | bytes 4194304 | tf_op jit(solution)/shard_map/all_to_all | solution.py:488
